TPU v7x, 256 devices: a whole 4x4x8 slice. The times are simulated.
256 devices in a mesh: tensor: 8 (over z), expert: 32 (over y, x, core).
Axes of the slice: x: 4, y: 4, z: 8, core: 2. Of those that a mesh axis runs over, the one named last changes fastest.
Arguments:
- tokens: bfloat16 [4096, 7168], P('expert', 'tensor'), may hold values from -6 to 6
- route_ids: int32 [4096, 2], P('expert'), may hold values from 0 to 31, all different within a row; in each aligned block of 128 rows (0 to 127, 128 to 255, ...) at most 16 rows name the same one
- route_weights: float32 [4096, 2], P('expert'), may hold values from 0.1 to 1
- cotangent: bfloat16 [4096, 7168], P('expert', 'tensor'), may hold values from -6 to 6
- w_gate: bfloat16 [32, 7168, 1024], P('expert', None, 'tensor'), may hold values from -0.0625 to 0.0625
- w_up: bfloat16 [32, 7168, 1024], P('expert', None, 'tensor'), may hold values from -0.0625 to 0.0625
- w_down: bfloat16 [32, 1024, 7168], P('expert', 'tensor'), may hold values from -0.1875 to 0.1875
Outputs:
- mixed: bfloat16 [4096, 7168], P('expert', 'tensor')
- grad_tokens: bfloat16 [4096, 7168], P('expert', 'tensor')
- grad_route: float32 [4096, 2], P('expert')
- grad_gate: bfloat16 [32, 7168, 1024], P('expert', None, 'tensor')
- grad_up: bfloat16 [32, 7168, 1024], P('expert', None, 'tensor')
- grad_down: bfloat16 [32, 1024, 7168], P('expert', 'tensor')
Inputs may be any that keep to these rules, and one draw needn't show every extreme that they name: `route_ids`: each row names 2 different experts. In each aligned block of 128 rows (the rows of one device) no expert is named by more than 16 rows, and in some block one expert is named by exactly 16 rows.
All inputs are finite; a program needn't handle non-finite values.
Results may differ from a plain program's by a relative error of at most 0.015.
Values may be sent and summed in bfloat16 or wider, within the bound.
A program may use at most 128 MiB of HBM per device.

v0:
```python
import jax
import jax.numpy as jnp
from jax import lax
from jax.sharding import PartitionSpec as P

TOPK = 2


ROW_PAIRS = (((1,), (1,)), ((), ()))
COLUMN_PAIRS = (((0,), (0,)), ((), ()))


def slot_tables(route_ids, experts, capacity):
    pair_count = route_ids.shape[0] * route_ids.shape[1]
    flat_ids = route_ids.reshape(pair_count)
    labels = jnp.arange(experts, dtype=jnp.int32)
    onehot = (flat_ids[:, None] == labels[None, :]).astype(jnp.int32)
    before = jnp.cumsum(onehot, axis=0) - onehot
    slot_index = jnp.sum(before * onehot, axis=1)
    target = flat_ids * capacity + slot_index
    source = (
        jnp.full((experts * capacity,), pair_count, jnp.int32)
        .at[target]
        .set(jnp.arange(pair_count, dtype=jnp.int32))
    )
    return (target, source)


def fill_slots(token_part, cot_part, weight_flat, source):
    row_of = source // TOPK
    zero_row = jnp.zeros((1, token_part.shape[1]), jnp.bfloat16)
    padded_tokens = jnp.concatenate([token_part, zero_row], axis=0)
    padded_cot = jnp.concatenate([cot_part, zero_row], axis=0)
    padded_weight = jnp.concatenate([weight_flat, jnp.zeros((1,), jnp.float32)], axis=0)
    token_slots = padded_tokens[row_of]
    cot_slots = (padded_weight[source][:, None] * padded_cot[row_of].astype(jnp.float32)).astype(
        jnp.bfloat16
    )
    return (token_slots, cot_slots)


def local(tokens, route_ids, route_weights, cotangent, w_gate, w_up, w_down):
    experts = lax.axis_size("expert")
    tok_rows, slice_width = tokens.shape
    capacity = 4 * tok_rows // experts
    gate_matrix = w_gate[0]
    up_matrix = w_up[0]
    down_weight = w_down[0]
    target, source = slot_tables(route_ids, experts, capacity)
    weight_flat = route_weights.reshape(tok_rows * TOPK)
    full_tokens, full_cot = (
        lax.all_gather(tokens, "tensor", axis=1, tiled=True),
        lax.all_gather(cotangent, "tensor", axis=1, tiled=True),
    )
    model_width = full_tokens.shape[1]
    token_slots, cot_slots = fill_slots(full_tokens, full_cot, weight_flat, source)
    routed, routed_cot = (
        lax.all_to_all(
            token_slots.reshape(experts, capacity, model_width),
            "expert",
            split_axis=0,
            concat_axis=0,
            tiled=True,
        ),
        lax.all_to_all(
            cot_slots.reshape(experts, capacity, model_width),
            "expert",
            split_axis=0,
            concat_axis=0,
            tiled=True,
        ),
    )
    routed = routed.reshape(experts * capacity, model_width)
    routed_cot = routed_cot.reshape(experts * capacity, model_width)
    gate_proj = jnp.dot(routed, gate_matrix, preferred_element_type=jnp.float32)
    up_proj = jnp.dot(routed, up_matrix, preferred_element_type=jnp.float32)
    hidden_state = (jax.nn.silu(gate_proj) * up_proj).astype(jnp.bfloat16)
    down_part = jnp.dot(hidden_state, down_weight, preferred_element_type=jnp.float32)
    expert_sum = lax.psum_scatter(
        down_part.astype(jnp.bfloat16), "tensor", scatter_dimension=1, tiled=True
    )
    expert_output = expert_sum.reshape(experts, capacity, slice_width)
    returned = lax.all_to_all(
        expert_output, "expert", split_axis=0, concat_axis=0, tiled=True
    ).reshape(experts * capacity, slice_width)
    chosen = returned[target].astype(jnp.float32).reshape(tok_rows, TOPK, slice_width)
    mixed = jnp.sum(route_weights[:, :, None] * chosen, axis=1).astype(jnp.bfloat16)
    route_part = jnp.sum(cotangent.astype(jnp.float32)[:, None, :] * chosen, axis=2)
    grad_route = lax.psum(route_part, "tensor")
    d_hidden = lax.dot_general(
        routed_cot, down_weight, ROW_PAIRS, preferred_element_type=jnp.float32
    )
    grad_down = lax.dot_general(
        hidden_state, routed_cot, COLUMN_PAIRS, preferred_element_type=jnp.float32
    ).astype(jnp.bfloat16)
    sigmoid_gate = jax.nn.sigmoid(gate_proj)
    gate_gradient = (
        d_hidden * up_proj * sigmoid_gate * (1.0 + gate_proj * (1.0 - sigmoid_gate))
    ).astype(jnp.bfloat16)
    up_gradient = (d_hidden * jax.nn.silu(gate_proj)).astype(jnp.bfloat16)
    grad_gate = lax.dot_general(
        routed, gate_gradient, COLUMN_PAIRS, preferred_element_type=jnp.float32
    ).astype(jnp.bfloat16)
    grad_up = lax.dot_general(
        routed, up_gradient, COLUMN_PAIRS, preferred_element_type=jnp.float32
    ).astype(jnp.bfloat16)
    back_part = lax.dot_general(
        gate_gradient, gate_matrix, ROW_PAIRS, preferred_element_type=jnp.float32
    )
    back_part = back_part + lax.dot_general(
        up_gradient, up_matrix, ROW_PAIRS, preferred_element_type=jnp.float32
    )
    input_sum = lax.psum_scatter(
        back_part.astype(jnp.bfloat16), "tensor", scatter_dimension=1, tiled=True
    )
    input_rows = input_sum.reshape(experts, capacity, slice_width)
    returned_grads = lax.all_to_all(
        input_rows, "expert", split_axis=0, concat_axis=0, tiled=True
    ).reshape(experts * capacity, slice_width)
    chosen_grads = returned_grads[target].astype(jnp.float32).reshape(tok_rows, TOPK, slice_width)
    grad_tokens = jnp.sum(route_weights[:, :, None] * chosen_grads, axis=1).astype(jnp.bfloat16)
    return (mixed, grad_tokens, grad_route, grad_gate[None], grad_up[None], grad_down[None])


def solution(mesh):
    placed = (
        P("expert", "tensor"),
        P("expert", None),
        P("expert", None),
        P("expert", "tensor"),
        P("expert", None, "tensor"),
        P("expert", None, "tensor"),
        P("expert", "tensor", None),
    )
    return jax.shard_map(
        local,
        mesh=mesh,
        in_specs=placed,
        out_specs=(
            P("expert", "tensor"),
            P("expert", "tensor"),
            P("expert", None),
            P("expert", None, "tensor"),
            P("expert", None, "tensor"),
            P("expert", "tensor", None),
        ),
        check_vma=False,
    )
```

profile of v0, /device:TPU:2, one launch (start us, length us, event | category | flops | bytes accessed | tf_op | source)
XLA Modules:
  0.0 523.5 jit_solution(14123120934310768559)
XLA Ops:
  12.3 40.9 %all-gather.3.cloned.1.call-done = bf16[128,7168]{1,0:T(8,128)(2,1)} async-done(((bf16[128,896]{1,0:T(8,128)(2,1)}), bf16[128,7168]{1,0:T(8,128)(2,1)}) %all-gather.3.cloned.1.call-update) | async-done | bytes 1835024 | tf_op jit(solution)/shard_map/all_gather | solution.py:52
  53.2 3.0 concatenate.9
  56.2 15.6 %gather_fusion = bf16[512,7168]{1,0:T(8,128)(2,1)} fusion(bf16[129,7168]{1,0:T(8,128)(2,1)} %concatenate.9, s32[1024]{0:T(1024)S(1)} %pad_clamp_fusion.2), kind=kCustom, calls=%fused_computation | custom fusion | bytes 14682112 | tf_op jit(solution)/shard_map/gather | solution.py:35
  71.8 7.6 %all-to-all-start = ((bf16[32,16,7168]{2,1,0:T(8,128)(2,1)}), bf16[32,16,7168]{2,1,0:T(8,128)(2,1)}, u32[]{:S(2)}, u32[]{:S(2)}) async-start(bf16[32,16,7168]{2,1,0:T(8,128)(2,1)} %bitcast.70), calls=%async_computation | async-start | bytes 14680064 | tf_op jit(solution)/shard_map/all_to_all | solution.py:58
  80.5 3.5 gather_fusion.2
  84.1 37.0 %all-gather.5.cloned.1.call-done = bf16[128,7168]{1,0:T(8,128)(2,1)} async-done(((bf16[128,896]{1,0:T(8,128)(2,1)}), bf16[128,7168]{1,0:T(8,128)(2,1)}) %all-gather.5.cloned.1.call-update) | async-done | bytes 1835024 | tf_op jit(solution)/shard_map/all_gather | solution.py:53
  121.0 3.0 concatenate.11
  124.0 15.5 %gather_fusion.3 = bf16[512,7168]{1,0:T(8,128)(2,1)} fusion(bf16[129,7168]{1,0:T(8,128)(2,1)} %concatenate.11, s32[1024]{0:T(1024)S(1)} %pad_clamp_fusion.2), kind=kCustom, calls=%fused_computation.3 | custom fusion | bytes 14682112 | tf_op jit(solution)/shard_map/gather | solution.py:36
  139.6 8.6 %fusion = bf16[32,16,7168]{2,1,0:T(8,128)(2,1)} fusion(bf16[32,16,7168]{2,1,0:T(8,128)(2,1)} %bitcast.71, f32[32,16]{1,0:T(8,128)S(1)} %mul.87), kind=kLoop, calls=%fused_computation.7 | loop fusion | flops 11010048 | bytes 14682112 | tf_op jit(solution)/shard_map/convert_element_type | solution.py:36
  148.2 18.6 %all-to-all-done = bf16[32,16,7168]{2,1,0:T(8,128)(2,1)} async-done(((bf16[32,16,7168]{2,1,0:T(8,128)(2,1)}), bf16[32,16,7168]{2,1,0:T(8,128)(2,1)}, u32[]{:S(2)}, u32[]{:S(2)}) %all-to-all-start) | async-done | bytes 7340064 | tf_op jit(solution)/shard_map/all_to_all | solution.py:58
  166.8 9.4 %all-to-all-start.2 = ((bf16[32,16,7168]{2,1,0:T(8,128)(2,1)}), bf16[32,16,7168]{2,1,0:T(8,128)(2,1)}, u32[]{:S(2)}, u32[]{:S(2)}) async-start(bf16[32,16,7168]{2,1,0:T(8,128)(2,1)} %fusion), calls=%async_computation.2 | async-start | bytes 14680064 | tf_op jit(solution)/shard_map/all_to_all | solution.py:65
  176.4 5.8 %fusion.8 = f32[512,128]{1,0:T(8,128)S(1)} fusion(bf16[512,7168]{1,0:T(8,128)(2,1)} %bitcast.4, bf16[1,7168,128]{2,1,0:T(8,128)(2,1)} %param.12), kind=kOutput, calls=%fused_computation.20 | convolution fusion | flops 939524096 | bytes 9437184 | tf_op jit(solution)/shard_map/dot_general | solution.py:76
  182.2 5.2 fusion.12
  187.4 76.3 %all-to-all-done.2 = bf16[32,16,7168]{2,1,0:T(8,128)(2,1)} async-done(((bf16[32,16,7168]{2,1,0:T(8,128)(2,1)}), bf16[32,16,7168]{2,1,0:T(8,128)(2,1)}, u32[]{:S(2)}, u32[]{:S(2)}) %all-to-all-start.2) | async-done | bytes 7340064 | tf_op jit(solution)/shard_map/all_to_all | solution.py:65
  263.6 5.1 multiply_convert_fusion
  268.8 5.0 convolution_convert_fusion
  273.8 10.4 %copy.27 = bf16[512,7168]{0,1:T(8,128)(2,1)} copy(bf16[512,7168]{1,0:T(8,128)(2,1)} %convolution_convert_fusion) | data formatting | bytes 14680064
  284.3 8.9 %fusion.10 = f32[512,7168]{1,0:T(8,128)} fusion(bf16[512,128]{1,0:T(8,128)(2,1)S(1)} %get-tuple-element.16, bf16[1,7168,128]{2,1,0:T(8,128)(2,1)} %param.11), kind=kOutput, calls=%fused_computation.22 | convolution fusion | flops 939524096 | bytes 16646144 | tf_op jit(solution)/shard_map/dot_general | solution.py:107
  293.3 10.9 %add_convert_fusion = bf16[512,7168]{1,0:T(8,128)(2,1)} fusion(f32[512,7168]{1,0:T(8,128)} %fusion.10, bf16[512,128]{1,0:T(8,128)(2,1)S(1)} %get-tuple-element.15, bf16[1,7168,128]{2,1,0:T(8,128)(2,1)S(1)} %copy-done.1), kind=kOutput, calls=%fused_computation.8 | convolution fusion | flops 946864128 | bytes 23986176 | tf_op jit(solution)/shard_map/dot_general | solution.py:110
  304.2 10.5 %copy.29 = bf16[512,7168]{0,1:T(8,128)(2,1)} copy(bf16[512,7168]{1,0:T(8,128)(2,1)} %add_convert_fusion) | data formatting | bytes 14680064
  314.7 53.2 %reduce-scatter.7.cloned.1.call-done = bf16[896,512]{1,0:T(8,128)(2,1)} async-done(((bf16[7168,512]{1,0:T(8,128)(2,1)}), bf16[896,512]{1,0:T(8,128)(2,1)}) %reduce-scatter.7.cloned.1.call-update) | async-done | bytes 917520
  367.9 2.2 copy.28
  370.1 7.7 %all-to-all-start.1 = ((bf16[32,16,896]{2,1,0:T(8,128)(2,1)}), bf16[32,16,896]{2,1,0:T(8,128)(2,1)S(1)}, u32[]{:S(2)}, u32[]{:S(2)}) async-start(bf16[32,16,896]{2,1,0:T(8,128)(2,1)} %bitcast.76), calls=%async_computation.1 | async-start | bytes 1835008 | tf_op jit(solution)/shard_map/all_to_all | solution.py:83
  378.7 7.1 %fusion.2 = bf16[1,7168,128]{2,1,0:T(8,128)(2,1)} fusion(bf16[512,7168]{1,0:T(8,128)(2,1)} %bitcast.4, bf16[512,128]{1,0:T(8,128)(2,1)S(1)} %get-tuple-element.15), kind=kOutput, calls=%fused_computation.14 | convolution fusion | flops 940441600 | bytes 9306112 | tf_op jit(solution)/shard_map/dot_general | solution.py:104
  385.8 68.2 %reduce-scatter.9.cloned.1.call-done = bf16[896,512]{1,0:T(8,128)(2,1)} async-done(((bf16[7168,512]{1,0:T(8,128)(2,1)}), bf16[896,512]{1,0:T(8,128)(2,1)}) %reduce-scatter.9.cloned.1.call-update) | async-done | bytes 917520
  454.0 2.3 copy.30
  456.3 7.5 %all-to-all-start.3 = ((bf16[32,16,896]{2,1,0:T(8,128)(2,1)}), bf16[32,16,896]{2,1,0:T(8,128)(2,1)}, u32[]{:S(2)}, u32[]{:S(2)}) async-start(bf16[32,16,896]{2,1,0:T(8,128)(2,1)} %bitcast.75), calls=%async_computation.3 | async-start | bytes 1835008 | tf_op jit(solution)/shard_map/all_to_all | solution.py:117
  463.8 5.5 %fusion.3 = bf16[1,128,7168]{2,1,0:T(8,128)(2,1)} fusion(bf16[512,128]{1,0:T(8,128)(2,1)S(1)} %get-tuple-element.17, bf16[512,7168]{1,0:T(8,128)(2,1)} %bitcast.11), kind=kOutput, calls=%fused_computation.15 | convolution fusion | flops 940441600 | bytes 9306112 | tf_op jit(solution)/shard_map/dot_general | solution.py:93
  469.2 6.4 %fusion.1 = bf16[1,7168,128]{2,1,0:T(8,128)(2,1)} fusion(bf16[512,7168]{1,0:T(8,128)(2,1)} %bitcast.4, bf16[512,128]{1,0:T(8,128)(2,1)S(1)} %get-tuple-element.16), kind=kOutput, calls=%fused_computation.13 | convolution fusion | flops 940441600 | bytes 9306112 | tf_op jit(solution)/shard_map/dot_general | solution.py:101
  478.4 2.8 gather_fusion.4
  482.6 4.8 multiply_reduce_fusion
  487.4 28.7 %psum.7 = f32[128,2]{1,0:T(8,128)S(1)} all-reduce(f32[128,2]{1,0:T(8,128)S(1)} %get-tuple-element.12), channel_id=1, replica_groups=mesh['tensor'=8,'expert'=32] {'tensor'}, use_global_device_ids=true, to_apply=%region_9.10 | all-reduce | flops 256 | bytes 2048 | tf_op jit(solution)/shard_map/psum | solution.py:89
  (48 shorter events, 12.0 us)
Async XLA Ops:
  7.2 256.5 %copy-start = (bf16[1,128,7168]{2,1,0:T(8,128)(2,1)S(1)}, bf16[1,128,7168]{2,1,0:T(8,128)(2,1)}, u32[]{:S(2)}) copy-start(bf16[1,128,7168]{2,1,0:T(8,128)(2,1)} %param.13) | copy-start | bytes 5505028
  7.2 46.0 %all-gather.3.cloned.1.call-start = ((), (), s32[]{:S(2)}) async-start(), calls=%async_computation.6 | async-start | bytes 2064384 | tf_op jit(solution)/shard_map/all_gather | solution.py:52
  71.8 8.4 %copy-start.4 = (f32[128,2]{0,1:T(2,128)S(1)}, f32[128,2]{0,1:T(2,128)}, u32[]{:S(2)}) copy-start(f32[128,2]{0,1:T(2,128)} %param.9) | copy-start | bytes 3076
  71.8 94.9 %all-to-all-start = ((bf16[32,16,7168]{2,1,0:T(8,128)(2,1)}), bf16[32,16,7168]{2,1,0:T(8,128)(2,1)}, u32[]{:S(2)}, u32[]{:S(2)}) async-start(bf16[32,16,7168]{2,1,0:T(8,128)(2,1)} %bitcast.70), calls=%async_computation | async-start | bytes 14680064 | tf_op jit(solution)/shard_map/all_to_all | solution.py:58
  79.4 41.6 %all-gather.5.cloned.1.call-start = ((), (), s32[]{:S(2)}) async-start(), calls=%async_computation.7 | async-start | bytes 2064384 | tf_op jit(solution)/shard_map/all_gather | solution.py:53
  166.8 96.9 %all-to-all-start.2 = ((bf16[32,16,7168]{2,1,0:T(8,128)(2,1)}), bf16[32,16,7168]{2,1,0:T(8,128)(2,1)}, u32[]{:S(2)}, u32[]{:S(2)}) async-start(bf16[32,16,7168]{2,1,0:T(8,128)(2,1)} %fusion), calls=%async_computation.2 | async-start | bytes 14680064 | tf_op jit(solution)/shard_map/all_to_all | solution.py:65
  176.2 191.7 %reduce-scatter.7.cloned.1.call-start = ((), (), s32[]{:S(2)}) async-start(), calls=%async_computation.8 | async-start | bytes 8257536
  176.4 5.8 %copy-start.2 = (bf16[1,7168,128]{2,1,0:T(8,128)(2,1)S(1)}, bf16[1,7168,128]{2,1,0:T(8,128)(2,1)}, u32[]{:S(2)}) copy-start(bf16[1,7168,128]{2,1,0:T(8,128)(2,1)} %param.11) | copy-start | bytes 5505028
  284.3 169.8 %reduce-scatter.9.cloned.1.call-start = ((), (), s32[]{:S(2)}) async-start(), calls=%async_computation.9 | async-start | bytes 8257536
  284.3 8.9 %copy-start.1 = (bf16[1,7168,128]{2,1,0:T(8,128)(2,1)S(1)}, bf16[1,7168,128]{2,1,0:T(8,128)(2,1)}, u32[]{:S(2)}) copy-start(bf16[1,7168,128]{2,1,0:T(8,128)(2,1)} %param.12) | copy-start | bytes 5505028
  314.7 63.2 %copy-start.3 = (bf16[128,896]{1,0:T(8,128)(2,1)S(1)}, bf16[128,896]{1,0:T(8,128)(2,1)}, u32[]{:S(2)}) copy-start(bf16[128,896]{1,0:T(8,128)(2,1)} %param.10) | copy-start | bytes 688132
  370.1 86.1 %all-to-all-start.1 = ((bf16[32,16,896]{2,1,0:T(8,128)(2,1)}), bf16[32,16,896]{2,1,0:T(8,128)(2,1)S(1)}, u32[]{:S(2)}, u32[]{:S(2)}) async-start(bf16[32,16,896]{2,1,0:T(8,128)(2,1)} %bitcast.76), calls=%async_computation.1 | async-start | bytes 1835008 | tf_op jit(solution)/shard_map/all_to_all | solution.py:83
  456.3 22.1 %all-to-all-start.3 = ((bf16[32,16,896]{2,1,0:T(8,128)(2,1)}), bf16[32,16,896]{2,1,0:T(8,128)(2,1)}, u32[]{:S(2)}, u32[]{:S(2)}) async-start(bf16[32,16,896]{2,1,0:T(8,128)(2,1)} %bitcast.75), calls=%async_computation.3 | async-start | bytes 1835008 | tf_op jit(solution)/shard_map/all_to_all | solution.py:117
Sparse Core Ops, SparseCore 0:
  9.8 43.3 all-gather.2
  82.1 38.9 all-gather.4
  284.4 83.5 reduce-scatter.6
  370.3 83.6 reduce-scatter.8
where the time goes:
time: 531 us; the launch traced here: 523 us
  waiting for transfers between devices  296 us (56%)
  local copies, waits for them, and re-layouts  75.8 us (14%)
  matrix products  60 us (11%)
  starting transfers between devices  33 us (6%)
  blocking collectives  28.7 us (5%)
  other arithmetic  15.6 us (3%)
  between operations  14.2 us (3%)
    unnamed x6, waiting for transfers between devices  122 us
    all_to_all x1, waiting for transfers between devices, local(): lax.all_to_all(cot_slots.reshape(experts, capacity, model_width), 'expert...  76.3 us
    all_gather x1, waiting for transfers between devices, local(): lax.all_gather(tokens, 'tensor', axis=1, tiled=True)  40.9 us
    all_gather x1, waiting for transfers between devices, local(): lax.all_gather(cotangent, 'tensor', axis=1, tiled=True)  37 us
    psum x1, blocking collectives, local(): grad_route = lax.psum(route_part, 'tensor')  28.7 us
    unnamed x17, local copies, waits for them, and re-layouts  26.9 us
    all_to_all x1, waiting for transfers between devices, local(): lax.all_to_all(token_slots.reshape(experts, capacity, model_width), 'expe...  18.6 us
    gather x1, local copies, waits for them, and re-layouts, fill_slots(): token_slots = padded_tokens[row_of]  15.6 us
  transfers between devices with their start and end apart: 8, of which 7 were waited for; matrix products, arithmetic and copies ran while one was open for 20% of the time, Pallas kernels for 0%

commit v1 on v0

v1 whole, which is shorter than its diff:
```python
import functools

import jax
import jax.numpy as jnp
from jax import lax
from jax.experimental import pallas as pl
from jax.experimental.pallas import tpu as pltpu
from jax.sharding import PartitionSpec as P

MESH = pl.DeviceIdType.MESH
F32 = jnp.float32
BF16 = jnp.bfloat16
NT_DIMS = (((1,), (1,)), ((), ()))
VMEM = pl.BlockSpec(memory_space=pltpu.VMEM)
ANY = pl.BlockSpec(memory_space=pl.ANY)


def remote(src, dst, send, recv, **where):
    return pltpu.make_async_remote_copy(
        src_ref=src, dst_ref=dst, send_sem=send, recv_sem=recv, device_id=where, device_id_type=MESH
    )


def wait_bytes(ref, sem):
    pltpu.make_async_copy(ref, ref, sem).wait()


def slot_rows(ids_col, ids_row, cap):
    n = ids_row.shape[1]
    earlier = lax.broadcasted_iota(jnp.int32, (n, n), 0) < lax.broadcasted_iota(jnp.int32, (n, n), 1)
    same_row = lax.broadcasted_iota(jnp.int32, (n, n), 0) == lax.broadcasted_iota(jnp.int32, (n, n), 1)
    targets = []
    for k in range(2):
        mine = ids_row[k : k + 1, :]
        count = jnp.zeros((1, n), F32)
        for other in range(2):
            before = earlier | same_row if other < k else earlier
            hit = (ids_col[:, other : other + 1] == mine) & before
            count = count + jnp.sum(jnp.where(hit, 1.0, 0.0), axis=0, keepdims=True)
        targets.append(mine.astype(F32) * cap + count)
    return targets


def slot_cols(ids_col, ids_row, cap):
    n = ids_row.shape[1]
    earlier = lax.broadcasted_iota(jnp.int32, (n, n), 1) < lax.broadcasted_iota(jnp.int32, (n, n), 0)
    same_row = lax.broadcasted_iota(jnp.int32, (n, n), 0) == lax.broadcasted_iota(jnp.int32, (n, n), 1)
    targets = []
    for k in range(2):
        mine = ids_col[:, k : k + 1]
        count = jnp.zeros((n, 1), F32)
        for other in range(2):
            before = earlier | same_row if other < k else earlier
            hit = (ids_row[other : other + 1, :] == mine) & before
            count = count + jnp.sum(jnp.where(hit, 1.0, 0.0), axis=1, keepdims=True)
        targets.append(mine.astype(F32) * cap + count)
    return targets


def greet(nx, nz, me, t):
    barrier = pltpu.get_barrier_semaphore()

    def hello(i, _):
        pl.semaphore_signal(
            barrier, inc=1, device_id={"expert": lax.rem(me + i, nx), "tensor": t}, device_id_type=MESH
        )
        return 0

    lax.fori_loop(1, nx, hello, 0)
    for step in (1, nz - 1):
        pl.semaphore_signal(
            barrier, inc=1, device_id={"expert": me, "tensor": lax.rem(t + step, nz)}, device_id_type=MESH
        )
    return barrier


PIECES = 2


def dispatch_kernel(
    nx, nz, cap,
    ids_col_ref, ids_row_ref, weight_ref, tok_ref, cot_ref,
    routed_ref, rcot_ref,
    sel_ref, tokbuf, tslots, cslots,
    ring_send, ring_recv, push_send, push_recv, self_sem, cpush_send, cpush_recv, cself_sem,
    cring_send, cring_recv,
):
    me, t = lax.axis_index("expert"), lax.axis_index("tensor")
    rows = nx * cap
    n_tok = tok_ref.shape[0]
    right, left = lax.rem(t + 1, nz), lax.rem(t + nz - 1, nz)
    barrier = greet(nx, nz, me, t)

    t0, t1 = slot_rows(ids_col_ref[...], ids_row_ref[...], cap)
    w0, w1 = weight_ref[0:1, :], weight_ref[1:2, :]
    tile = 128

    def select(i, _):
        r = pl.ds(pl.multiple_of(i * tile, tile), tile)
        at = (lax.broadcasted_iota(jnp.int32, (tile, n_tok), 0) + i * tile).astype(F32)
        hit0, hit1 = at == t0, at == t1
        sel = jnp.where(hit0 | hit1, 1.0, 0.0).astype(BF16)
        sel_ref[r, :] = sel
        w = jnp.sum(jnp.where(hit0, w0, 0.0) + jnp.where(hit1, w1, 0.0), axis=1, keepdims=True)
        cslots[r, :] = (w * jnp.dot(sel, cot_ref[...], preferred_element_type=F32)).astype(BF16)
        return 0

    lax.fori_loop(0, rows // tile, select, 0)

    def fill(o, block):
        def body(i, _):
            r = pl.ds(pl.multiple_of(i * tile, tile), tile)
            tslots[o, r, :] = jnp.dot(sel_ref[r, :], block[...], preferred_element_type=F32).astype(BF16)
            return 0

        lax.fori_loop(0, rows // tile, body, 0)

    fill(t, tok_ref)
    pl.semaphore_wait(barrier, nx + 1)

    def slab(e):
        return pl.ds(pl.multiple_of(e * cap, cap), cap)

    def ring_right(k):
        o = lax.rem(t + nz - k, nz)
        return remote(
            tok_ref if k == 0 else tokbuf.at[o], tokbuf.at[o], ring_send.at[0, k], ring_recv.at[0, k],
            expert=me, tensor=right,
        )

    def ring_left(k):
        o = lax.rem(t + k, nz)
        return remote(
            tok_ref if k == 0 else tokbuf.at[o], tokbuf.at[o], ring_send.at[1, k], ring_recv.at[1, k],
            expert=me, tensor=left,
        )

    hops_right, hops_left = nz // 2, nz - 1 - nz // 2
    started = [ring_right(0), ring_left(0)]
    for c in started:
        c.start()

    def push_cot(i, _):
        p = lax.rem(me + i, nx)
        remote(cslots.at[slab(p)], rcot_ref.at[t, slab(me)], cpush_send, cpush_recv, expert=p, tensor=t).start()
        return 0

    lax.fori_loop(1, nx, push_cot, 0)
    own_cot = pltpu.make_async_copy(cslots.at[slab(me)], rcot_ref.at[t, slab(me)], cself_sem)
    own_cot.start()

    def push_tok(o, k):
        def body(i, _):
            p = lax.rem(me + i, nx)
            remote(
                tslots.at[o, slab(p)], routed_ref.at[o, slab(me)], push_send.at[k], push_recv.at[k],
                expert=p, tensor=t,
            ).start()
            return 0

        lax.fori_loop(1, nx, body, 0)
        own = pltpu.make_async_copy(tslots.at[o, slab(me)], routed_ref.at[o, slab(me)], self_sem.at[k])
        own.start()
        return own

    def cot_right(k, p):
        o = lax.rem(t + nz - k, nz)
        size = rows // 2 // PIECES
        r = pl.ds(p * size, size)
        return remote(
            rcot_ref.at[o, r], rcot_ref.at[o, r], cring_send.at[0, k, p], cring_recv.at[0, k, p],
            expert=me, tensor=right,
        )

    def cot_left(k, p):
        o = lax.rem(t + k, nz)
        size = rows // 2 // PIECES
        r = pl.ds(rows // 2 + p * size, size)
        return remote(
            rcot_ref.at[o, r], rcot_ref.at[o, r], cring_send.at[1, k, p], cring_recv.at[1, k, p],
            expert=me, tensor=left,
        )

    owns = [push_tok(t, 0)]

    def token_step(k):
        got = [(ring_right, k, lax.rem(t + nz - k, nz), hops_right, k)]
        if k <= hops_left:
            got.append((ring_left, k, lax.rem(t + k, nz), hops_left, nz - k))
        for make, k, o, hops, index in got:
            make(k - 1).wait_recv()
            if k < hops:
                c = make(k)
                c.start()
                started.append(c)
        for make, k, o, hops, index in got:
            fill(o, tokbuf.at[o])
            owns.append(push_tok(o, index))

    def cot_step(k):
        for p in range(PIECES):
            for make in (cot_right, cot_left):
                if k > 0:
                    make(k - 1, p).wait_recv()
                if k < nz - 1:
                    c = make(k, p)
                    c.start()
                    started.append(c)

    token_step(1)
    wait_bytes(rcot_ref.at[0, pl.ds(0, rows - cap)], cpush_recv)
    own_cot.wait()
    cot_step(0)
    for k in range(2, hops_right + 1):
        token_step(k)
        cot_step(k - 1)
    for k in range(hops_right, nz):
        cot_step(k)

    for k in range(nz):
        owns[k].wait()
        wait_bytes(tslots.at[0, pl.ds(0, rows - cap)], push_send.at[k])
        wait_bytes(tslots.at[0, pl.ds(0, rows - cap)], push_recv.at[k])
    wait_bytes(cslots.at[pl.ds(0, rows - cap)], cpush_send)
    for c in started:
        c.wait_send()


def dispatch(nx, nz, cap, ids, ids_t, weights_t, tokens, cotangent):
    n_tok, width = tokens.shape
    rows = nx * cap
    dma = pltpu.SemaphoreType.DMA
    out = jax.ShapeDtypeStruct((nz, rows, width), BF16)
    return pl.pallas_call(
        functools.partial(dispatch_kernel, nx, nz, cap),
        out_shape=(out, out),
        in_specs=[VMEM] * 5,
        out_specs=(ANY, ANY),
        scratch_shapes=[
            pltpu.VMEM((rows, n_tok), BF16),
            pltpu.VMEM((nz, n_tok, width), BF16),
            pltpu.VMEM((nz, rows, width), BF16),
            pltpu.VMEM((rows, width), BF16),
            dma((2, nz // 2)), dma((2, nz // 2)), dma((nz,)), dma((nz,)), dma((nz,)), dma, dma, dma,
            dma((2, nz - 1, PIECES)), dma((2, nz - 1, PIECES)),
        ],
        compiler_params=pltpu.CompilerParams(
            collective_id=0, has_side_effects=True, vmem_limit_bytes=60 * 1024 * 1024
        ),
        name="dispatch",
    )(ids, ids_t, weights_t, tokens, cotangent)


def hidden_kernel(routed_ref, rcot_ref, wg_ref, wu_ref, wd_ref, hid_ref, dgu_ref, dot_ref, gu_acc, dh_acc):
    o = pl.program_id(0)
    w = jnp.concatenate([wg_ref[...], wu_ref[...]], axis=1)
    gu = jnp.dot(routed_ref[0], w, preferred_element_type=F32)
    dh = lax.dot_general(rcot_ref[0], wd_ref[...], NT_DIMS, preferred_element_type=F32)

    @pl.when(o == 0)
    def _():
        gu_acc[...] = gu
        dh_acc[...] = dh

    @pl.when(o > 0)
    def _():
        gu_acc[...] += gu
        dh_acc[...] += dh

    @pl.when(o == pl.num_programs(0) - 1)
    def _():
        h = dh_acc.shape[1]
        gate, up, d_hidden = gu_acc[:, :h], gu_acc[:, h:], dh_acc[...]
        sig = 1.0 / (1.0 + jnp.exp(-gate))
        silu = gate * sig
        hidden = (silu * up).astype(BF16)
        hid_ref[...] = hidden
        d_gate = d_hidden * up * sig * (1.0 + gate * (1.0 - sig))
        dgu_ref[...] = jnp.concatenate([d_gate.astype(BF16), (d_hidden * silu).astype(BF16)], axis=1)
        dot_ref[...] = jnp.sum(hidden.astype(F32) * d_hidden, axis=1, keepdims=True)


def hidden_stage(routed, rcot, wg, wu, wd):
    nz, rows, width = routed.shape
    h = wg.shape[1]
    block = pl.BlockSpec((1, rows, width), lambda o: (o, 0, 0))
    wspec = pl.BlockSpec((width, h), lambda o: (o, 0))
    return pl.pallas_call(
        hidden_kernel,
        grid=(nz,),
        out_shape=(
            jax.ShapeDtypeStruct((rows, h), BF16),
            jax.ShapeDtypeStruct((rows, 2 * h), BF16),
            jax.ShapeDtypeStruct((rows, 1), F32),
        ),
        in_specs=[block, block, wspec, wspec, pl.BlockSpec((h, width), lambda o: (0, o))],
        out_specs=[
            pl.BlockSpec((rows, h), lambda o: (0, 0)),
            pl.BlockSpec((rows, 2 * h), lambda o: (0, 0)),
            pl.BlockSpec((rows, 1), lambda o: (0, 0)),
        ],
        scratch_shapes=[pltpu.VMEM((rows, 2 * h), F32), pltpu.VMEM((rows, h), F32)],
        name="hidden",
    )(routed, rcot, wg, wu, wd)


def parts_kernel(hid_ref, dgu_ref, wg_ref, wu_ref, wd_ref, down_ref, back_ref):
    down_ref[0] = jnp.dot(hid_ref[...], wd_ref[...], preferred_element_type=F32).astype(BF16)
    w = jnp.concatenate([wg_ref[...], wu_ref[...]], axis=1)
    back_ref[0] = lax.dot_general(dgu_ref[...], w, NT_DIMS, preferred_element_type=F32).astype(BF16)


def parts_stage(nz, hid, dgu, wg, wu, wd):
    rows, h = hid.shape
    width = wg.shape[0] // nz
    out = jax.ShapeDtypeStruct((nz, rows, width), BF16)
    wspec = pl.BlockSpec((width, h), lambda o: (o, 0))
    block = pl.BlockSpec((1, rows, width), lambda o: (o, 0, 0))
    return pl.pallas_call(
        parts_kernel,
        grid=(nz,),
        out_shape=(out, out),
        in_specs=[
            pl.BlockSpec((rows, h), lambda o: (0, 0)),
            pl.BlockSpec((rows, 2 * h), lambda o: (0, 0)),
            wspec, wspec, pl.BlockSpec((h, width), lambda o: (0, o)),
        ],
        out_specs=(block, block),
        name="parts",
    )(hid, dgu, wg, wu, wd)


def grads_kernel(routed_ref, rcot_ref, hid_ref, dgu_ref, gg_ref, gu_ref, gd_ref, hid_t, dgu_t):
    @pl.when(pl.program_id(0) == 0)
    def _():
        hid_t[...] = hid_ref[...].astype(F32).T.astype(BF16)
        dgu_t[...] = dgu_ref[...].astype(F32).T.astype(BF16)

    h = hid_t.shape[0]
    gd_ref[...] = jnp.dot(hid_t[...], rcot_ref[0], preferred_element_type=F32).astype(BF16)
    both = jnp.dot(dgu_t[...], routed_ref[0], preferred_element_type=F32).T.astype(BF16)
    gg_ref[...] = both[:, :h]
    gu_ref[...] = both[:, h:]


def grads_stage(routed, rcot, hid, dgu):
    nz, rows, width = routed.shape
    h = hid.shape[1]
    block = pl.BlockSpec((1, rows, width), lambda o: (o, 0, 0))
    gspec = pl.BlockSpec((width, h), lambda o: (o, 0))
    return pl.pallas_call(
        grads_kernel,
        grid=(nz,),
        out_shape=(
            jax.ShapeDtypeStruct((nz * width, h), BF16),
            jax.ShapeDtypeStruct((nz * width, h), BF16),
            jax.ShapeDtypeStruct((h, nz * width), BF16),
        ),
        in_specs=[
            block, block,
            pl.BlockSpec((rows, h), lambda o: (0, 0)),
            pl.BlockSpec((rows, 2 * h), lambda o: (0, 0)),
        ],
        out_specs=(gspec, gspec, pl.BlockSpec((h, width), lambda o: (0, o))),
        scratch_shapes=[pltpu.VMEM((h, rows), BF16), pltpu.VMEM((2 * h, rows), BF16)],
        cost_estimate=pl.CostEstimate(
            flops=6 * nz * rows * width * h, bytes_accessed=4 * nz * rows * width + 6 * nz * width * h,
            transcendentals=0,
        ),
        name="grads",
    )(routed, rcot, hid, dgu)


def combine_kernel(cap, ids_col_ref, ids_row_ref, weight_ref, ret_ref, out_ref, pick):
    n = ids_col_ref.shape[0]
    rows = ret_ref.shape[1]

    @pl.when(pl.program_id(0) == 0)
    def _():
        at = lax.broadcasted_iota(jnp.int32, (n, rows), 1).astype(F32)
        for k, target in enumerate(slot_cols(ids_col_ref[...], ids_row_ref[...], cap)):
            pick[k * n : (k + 1) * n, :] = jnp.where(at == target, 1.0, 0.0).astype(BF16)

    chosen = jnp.dot(pick[...], ret_ref[0], preferred_element_type=F32)
    out_ref[0] = (weight_ref[:, 0:1] * chosen[:n] + weight_ref[:, 1:2] * chosen[n:]).astype(BF16)


def combine(cap, ids, ids_t, weights, ret):
    blocks, rows, width = ret.shape
    n = ids.shape[0]
    return pl.pallas_call(
        functools.partial(combine_kernel, cap),
        grid=(blocks,),
        out_shape=jax.ShapeDtypeStruct((blocks, n, width), BF16),
        in_specs=[
            pl.BlockSpec((n, 2), lambda o: (0, 0)),
            pl.BlockSpec((2, n), lambda o: (0, 0)),
            pl.BlockSpec((n, 2), lambda o: (0, 0)),
            pl.BlockSpec((1, rows, width), lambda o: (o, 0, 0)),
        ],
        out_specs=pl.BlockSpec((1, n, width), lambda o: (o, 0, 0)),
        scratch_shapes=[pltpu.VMEM((2 * n, rows), BF16)],
        name="combine",
    )(ids, ids_t, weights, ret)


def local(tokens, ids, weights, cotangent, w_gate, w_up, w_down):
    nx, nz = lax.axis_size("expert"), lax.axis_size("tensor")
    n_tok, width = tokens.shape
    cap = 4 * n_tok // nx
    ids_t, weights_t = ids.T, weights.T
    wg, wu, wd = w_gate[0], w_up[0], w_down[0]
    routed, rcot = dispatch(nx, nz, cap, ids, ids_t, weights_t, tokens, cotangent)
    hid, dgu, dots = hidden_stage(routed, rcot, wg, wu, wd)
    down, back = parts_stage(nz, hid, dgu, wg, wu, wd)

    returned = lax.all_to_all(
        down.reshape(nz, nx, cap, width), "expert", split_axis=1, concat_axis=1, tiled=True
    ).reshape(nz, nx * cap, width)
    input_rows = lax.psum_scatter(back, "tensor", scatter_dimension=0, tiled=True)
    dots_all = jnp.sum(lax.all_gather(dots[:, 0], "tensor", axis=0), axis=0)
    dots_back = lax.all_to_all(
        dots_all.reshape(nx, cap), "expert", split_axis=0, concat_axis=0, tiled=True
    ).reshape(nx * cap)
    ret_grads = lax.all_to_all(
        input_rows.reshape(nx, cap, width), "expert", split_axis=0, concat_axis=0, tiled=True
    ).reshape(1, nx * cap, width)
    grad_gate, grad_up, grad_down = grads_stage(routed, rcot, hid, dgu)
    mixed_parts = combine(cap, ids, ids_t, weights, returned)
    mixed = lax.psum_scatter(mixed_parts, "tensor", scatter_dimension=0, tiled=True)[0]
    grad_tokens = combine(cap, ids, ids_t, weights, ret_grads)[0]
    target = jnp.stack(slot_cols(ids, ids_t, cap), axis=1)[:, :, 0]
    at = jnp.arange(nx * cap, dtype=F32)
    grad_route = (
        jnp.sum(jnp.where(target[:, :, None] == at, dots_back, 0.0), axis=2) / weights
    )
    return (mixed, grad_tokens, grad_route, grad_gate[None], grad_up[None], grad_down[None])


def solution(mesh):
    placed = (
        P("expert", "tensor"),
        P("expert", None),
        P("expert", None),
        P("expert", "tensor"),
        P("expert", None, "tensor"),
        P("expert", None, "tensor"),
        P("expert", "tensor", None),
    )
    return jax.shard_map(
        local,
        mesh=mesh,
        in_specs=placed,
        out_specs=(
            P("expert", "tensor"),
            P("expert", "tensor"),
            P("expert", None),
            P("expert", None, "tensor"),
            P("expert", None, "tensor"),
            P("expert", "tensor", None),
        ),
        check_vma=False,
    )
```

time: 531 us -> 343 us (0.65)
  waiting for transfers between devices: 296 us -> 93.4 us
  Pallas kernels: 0 us -> 147 us
  matrix products: 60 us -> 0 us
  local copies, waits for them, and re-layouts: 75.8 us -> 18.2 us
  other arithmetic: 15.6 us -> 2.3 us
  blocking collectives: 28.7 us -> 39.3 us
  starting transfers between devices: 33 us -> 25.4 us
    pallas_call x0 -> x6, Pallas kernels: none -> 147 us  [the longest x1 101 us: dispatch(): pl.pallas_call(functools.partial(dispatch_kernel, nx, nz, cap), out_shape...]
    unnamed x6 -> x2, waiting for transfers between devices: 122 us -> 0.03 us
    all_gather x2 -> x0, waiting for transfers between devices: 77.8 us -> none  [the longest x1 40.9 us: local(): lax.all_gather(tokens, 'tensor', axis=1, tiled=True)]
    dot_general x9 -> x0, matrix products: 60 us -> none  [the longest x1 10.9 us: local(): lax.dot_general(up_gradient, up_matrix, ROW_PAIRS, preferred_element_type...]
    all_gather x0 -> x1, blocking collectives: none -> 39.3 us  [local(): dots_all = jnp.sum(lax.all_gather(dots[:, 0], 'tensor', axis=0), axis=0)]
    gather x5 -> x0, local copies, waits for them, and re-layouts: 38.6 us -> none  [the longest x1 15.6 us: fill_slots(): token_slots = padded_tokens[row_of]]
    psum x1 -> x0, blocking collectives: 28.7 us -> none  [local(): grad_route = lax.psum(route_part, 'tensor')]
    unnamed x17 -> x10, local copies, waits for them, and re-layouts: 26.9 us -> 3.08 us
  transfers between devices with their start and end apart: 8 -> 5, of which waited for: 7 -> 3; matrix products, arithmetic and copies ran while one was open for 20% -> 5% of each run, Pallas kernels for 0% -> 7%
where the time goes in v1:
time: 343 us; the launch traced here: 340 us
  Pallas kernels  147 us (43%)
  waiting for transfers between devices  93.4 us (27%)
  blocking collectives  39.3 us (11%)
  starting transfers between devices  25.4 us (7%)
  local copies, waits for them, and re-layouts  18.2 us (5%)
  between operations  14.2 us (4%)
    pallas_call x1, Pallas kernels, dispatch(): pl.pallas_call(functools.partial(dispatch_kernel, nx, nz, cap), out_shape...  101 us
    all_to_all x1, waiting for transfers between devices, local(): lax.all_to_all(down.reshape(nz, nx, cap, width), 'expert', split_axis=1,...  86.5 us
    all_gather x1, blocking collectives, local(): dots_all = jnp.sum(lax.all_gather(dots[:, 0], 'tensor', axis=0), axis=0)  39.3 us
    all_to_all x1, starting transfers between devices, local(): lax.all_to_all(down.reshape(nz, nx, cap, width), 'expert', split_axis=1,...  12.6 us
    pallas_call x1, Pallas kernels, hidden_stage(): pl.pallas_call(hidden_kernel, grid=(nz,), out_shape=(jax.ShapeDtypeStruct...  11.9 us
    pallas_call x1, Pallas kernels, parts_stage(): pl.pallas_call(parts_kernel, grid=(nz,), out_shape=(out, out), in_specs=[...  11.8 us
    pallas_call x1, Pallas kernels, grads_stage(): pl.pallas_call(grads_kernel, grid=(nz,), out_shape=(jax.ShapeDtypeStruct(...  11.7 us
    pallas_call x2, Pallas kernels, combine(): pl.pallas_call(functools.partial(combine_kernel, cap), grid=(blocks,), ou...  11.5 us
  transfers between devices with their start and end apart: 5, of which 3 were waited for; matrix products, arithmetic and copies ran while one was open for 5% of the time, Pallas kernels for 7%

profile of v1, /device:TPU:2, one launch (start us, length us, event | category | flops | bytes accessed | tf_op | source)
XLA Modules:
  0.0 340.3 jit_solution(12530700791702725356)
XLA Ops:
  7.2 0.0 reduce-scatter.5.cloned.1.call-start
  7.2 1.4 copy.37.ids_col_ref
  8.6 100.6 %dispatch.1 = (bf16[8,512,896]{2,1,0:T(8,128)(2,1)}, bf16[8,512,896]{2,1,0:T(8,128)(2,1)}) custom-call(s32[128,2]{1,0:T(8,128)} %copy.37.ids_col_ref, s32[2,128]{1,0:T(2,128)} %bitcast.47, f32[2,128]{1,0:T(2,128)} %bitcast.51, bf16[128,896]{1,0:T(8,128)(2,1)} %tok_ref.1, bf16[128,896]{1,0:T(8,128)(2,1)} %cot_ref.1), custom_call_target="tpu_custom_call" | custom-call | tf_op jit(solution)/shard_map/dispatch/pallas_call | solution.py:234
  109.2 11.9 %hidden.1 = (bf16[512,128]{1,0:T(8,128)(2,1)}, bf16[512,256]{1,0:T(8,128)(2,1)}, f32[512,1]{1,0:T(8,128)}) custom-call(bf16[8,512,896]{2,1,0:T(8,128)(2,1)} %get-tuple-element.16.routed_ref, bf16[8,512,896]{2,1,0:T(8,128)(2,1)} %get-tuple-element.17.rcot_ref, bf16[7168,128]{1,0:T(8,128)(2,1)} %bitcast.37, bf16[7168,128]{1,0:T(8,128)(2,1)} %bitcast.39, ...), custom_call_target="tpu_custom_call" | custom-call | tf_op jit(solution)/shard_map/hidden/pallas_call | solution.py:288
  121.2 11.8 %parts.1 = (bf16[8,512,896]{2,1,0:T(8,128)(2,1)}, bf16[8,512,896]{2,1,0:T(8,128)(2,1)}) custom-call(bf16[512,128]{1,0:T(8,128)(2,1)} %get-tuple-element.18.hid_ref, bf16[512,256]{1,0:T(8,128)(2,1)} %get-tuple-element.19.dgu_ref, bf16[7168,128]{1,0:T(8,128)(2,1)} %bitcast.38, bf16[7168,128]{1,0:T(8,128)(2,1)} %bitcast.40, bf16[128,7168]{1,0:T(8,128)(2,1)} %bitcast.42), custom_call_target="tpu_custom_call" | custom-call | tf_op jit(solution)/shard_map/parts/pallas_call | solution.py:319
  132.9 0.0 reduce-scatter.5.cloned.1.call-update
  133.0 7.1 %copy.35 = bf16[8,32,16,896]{3,2,0,1:T(8,128)(2,1)} copy(bf16[8,32,16,896]{3,2,1,0:T(8,128)(2,1)} %bitcast.43) | data formatting | bytes 14680064 | tf_op jit(solution)/shard_map/reshape | solution.py:418
  140.1 12.6 %all-to-all-start = ((bf16[8,32,16,896]{3,2,0,1:T(8,128)(2,1)}), bf16[8,32,16,896]{3,2,0,1:T(8,128)(2,1)}, u32[]{:S(2)}, u32[]{:S(2)}) async-start(bf16[8,32,16,896]{3,2,0,1:T(8,128)(2,1)} %copy.35), calls=%async_computation | async-start | bytes 14680064 | tf_op jit(solution)/shard_map/all_to_all | solution.py:417
  152.7 0.0 reduce-scatter.3.cloned.1.call-start
  152.7 0.0 copy-done.3
  152.7 0.7 copy.38.weight_ref
  153.5 86.5 %all-to-all-done = bf16[8,32,16,896]{3,2,0,1:T(8,128)(2,1)} async-done(((bf16[8,32,16,896]{3,2,0,1:T(8,128)(2,1)}), bf16[8,32,16,896]{3,2,0,1:T(8,128)(2,1)}, u32[]{:S(2)}, u32[]{:S(2)}) %all-to-all-start) | async-done | bytes 7340064 | tf_op jit(solution)/shard_map/all_to_all | solution.py:417
  240.0 6.7 %copy.36 = bf16[8,32,16,896]{3,2,1,0:T(8,128)(2,1)} copy(bf16[8,32,16,896]{3,2,0,1:T(8,128)(2,1)} %all-to-all-done) | data formatting | bytes 14680064 | tf_op jit(solution)/shard_map/all_to_all | solution.py:417
  246.7 8.7 %combine.2 = bf16[8,128,896]{2,1,0:T(8,128)(2,1)} custom-call(s32[128,2]{1,0:T(8,128)} %copy.37.ids_col_ref, s32[2,128]{1,0:T(2,128)} %bitcast.48, f32[128,2]{1,0:T(8,128)} %copy.38.weight_ref, bf16[8,512,896]{2,1,0:T(8,128)(2,1)} %bitcast.36), custom_call_target="tpu_custom_call" | custom-call | tf_op jit(solution)/shard_map/combine/pallas_call | solution.py:391
  255.4 0.0 reduce-scatter.3.cloned.1.call-update
  255.4 0.0 copy-start.2
  255.4 39.3 %all-gather = f32[4096,1]{1,0:T(8,128)S(1)} all-gather(f32[512,1]{1,0:T(8,128)S(1)} %copy-done.1), channel_id=2, replica_groups=mesh['tensor'=8,'expert'=32] {'tensor'}, dimensions={0}, use_global_device_ids=true | all-gather | bytes 18432 | tf_op jit(solution)/shard_map/all_gather | solution.py:421
  294.8 0.6 reduce
  295.4 0.7 all_to_all.14
  296.1 7.7 %all-to-all-start.2 = ((f32[32,1,16]{2,1,0:T(1,128)}), f32[32,1,16]{2,1,0:T(1,128)S(1)}, u32[]{:S(2)}, u32[]{:S(2)}) async-start(f32[32,1,16]{2,1,0:T(1,128)} %bitcast.20), calls=%async_computation.4 | async-start | bytes 32768 | tf_op jit(solution)/shard_map/all_to_all | solution.py:422
  303.8 6.2 %all-to-all-done.2 = f32[32,1,16]{2,1,0:T(1,128)S(1)} async-done(((f32[32,1,16]{2,1,0:T(1,128)}), f32[32,1,16]{2,1,0:T(1,128)S(1)}, u32[]{:S(2)}, u32[]{:S(2)}) %all-to-all-start.2) | async-done | bytes 2080 | tf_op jit(solution)/shard_map/all_to_all | solution.py:422
  310.0 5.0 %all-to-all-start.1 = ((bf16[32,16,896]{2,1,0:T(8,128)(2,1)}), bf16[32,16,896]{2,1,0:T(8,128)(2,1)S(1)}, u32[]{:S(2)}, u32[]{:S(2)}) async-start(bf16[32,16,896]{2,1,0:T(8,128)(2,1)} %bitcast.45), calls=%async_computation.3 | async-start | bytes 1835008 | tf_op jit(solution)/shard_map/all_to_all | solution.py:425
  315.1 0.2 select_reduce_fusion.3
  315.3 11.7 %grads.1 = (bf16[7168,128]{1,0:T(8,128)(2,1)}, bf16[7168,128]{1,0:T(8,128)(2,1)}, bf16[128,7168]{1,0:T(8,128)(2,1)}) custom-call(bf16[8,512,896]{2,1,0:T(8,128)(2,1)} %get-tuple-element.16.routed_ref, bf16[8,512,896]{2,1,0:T(8,128)(2,1)} %get-tuple-element.17.rcot_ref, bf16[512,128]{1,0:T(8,128)(2,1)} %get-tuple-element.18.hid_ref, ...), custom_call_target="tpu_custom_call" | custom-call | flops 2818572288 | bytes 20185088 | tf_op jit(solution)/shard_map/grads/pallas_call | solution.py:351
  327.0 0.5 broadcast.10
  327.5 0.7 reduce.4
  328.2 0.1 reshape.62
  328.3 0.2 select_reduce_fusion
  328.5 0.6 div.3
  329.1 0.7 all-to-all-done.1
  329.8 0.9 copy-done
  330.7 2.7 combine.3
  (13 shorter events, 0.1 us)
Async XLA Ops:
  7.2 302.9 %reduce-scatter.5.cloned.1.call-start = ((), (), s32[]{:S(2)}) async-start(), calls=%async_computation.6 | async-start | bytes 8257536 | tf_op jit(solution)/shard_map/reduce_scatter | solution.py:420
  140.1 12.6 %copy-start.3 = (f32[128,2]{0,1:T(2,128)S(1)}, f32[128,2]{0,1:T(2,128)}, u32[]{:S(2)}) copy-start(f32[128,2]{0,1:T(2,128)} %param.9) | copy-start | bytes 3076
  140.1 99.9 %all-to-all-start = ((bf16[8,32,16,896]{3,2,0,1:T(8,128)(2,1)}), bf16[8,32,16,896]{3,2,0,1:T(8,128)(2,1)}, u32[]{:S(2)}, u32[]{:S(2)}) async-start(bf16[8,32,16,896]{3,2,0,1:T(8,128)(2,1)} %copy.35), calls=%async_computation | async-start | bytes 14680064 | tf_op jit(solution)/shard_map/all_to_all | solution.py:417
  152.7 180.8 %reduce-scatter.3.cloned.1.call-start = ((), (), s32[]{:S(2)}) async-start(), calls=%async_computation.5 | async-start | bytes 2064384 | tf_op jit(solution)/shard_map/reduce_scatter | solution.py:430
  246.7 8.7 %copy-start.1 = (f32[512,1]{1,0:T(8,128)S(1)}, f32[512,1]{1,0:T(8,128)}, u32[]{:S(2)}) copy-start(f32[512,1]{1,0:T(8,128)} %get-tuple-element.22) | copy-start | bytes 6148
  255.4 48.4 %copy-start.2 = (s32[128,2]{0,1:T(2,128)S(1)}, s32[128,2]{0,1:T(2,128)}, u32[]{:S(2)}) copy-start(s32[128,2]{0,1:T(2,128)} %param.8) | copy-start | bytes 3076
  296.1 13.9 %all-to-all-start.2 = ((f32[32,1,16]{2,1,0:T(1,128)}), f32[32,1,16]{2,1,0:T(1,128)S(1)}, u32[]{:S(2)}, u32[]{:S(2)}) async-start(f32[32,1,16]{2,1,0:T(1,128)} %bitcast.20), calls=%async_computation.4 | async-start | bytes 32768 | tf_op jit(solution)/shard_map/all_to_all | solution.py:422
  310.0 19.7 %all-to-all-start.1 = ((bf16[32,16,896]{2,1,0:T(8,128)(2,1)}), bf16[32,16,896]{2,1,0:T(8,128)(2,1)S(1)}, u32[]{:S(2)}, u32[]{:S(2)}) async-start(bf16[32,16,896]{2,1,0:T(8,128)(2,1)} %bitcast.45), calls=%async_computation.3 | async-start | bytes 1835008 | tf_op jit(solution)/shard_map/all_to_all | solution.py:425
  329.8 0.9 copy-start
Sparse Core Ops, SparseCore 0:
  133.1 87.4 reduce-scatter.4
  255.5 45.0 reduce-scatter.2

commit v2 on v0

v2 whole, which is shorter than its diff:
```python
import functools

import jax
import jax.numpy as jnp
from jax import lax
from jax.experimental import pallas as pl
from jax.experimental.pallas import tpu as pltpu
from jax.sharding import PartitionSpec as P

MESH = pl.DeviceIdType.MESH
F32 = jnp.float32
BF16 = jnp.bfloat16
NT_DIMS = (((1,), (1,)), ((), ()))
VMEM = pl.BlockSpec(memory_space=pltpu.VMEM)
ANY = pl.BlockSpec(memory_space=pl.ANY)


def remote(src, dst, send, recv, **where):
    return pltpu.make_async_remote_copy(
        src_ref=src, dst_ref=dst, send_sem=send, recv_sem=recv, device_id=where, device_id_type=MESH
    )


def wait_bytes(ref, sem):
    pltpu.make_async_copy(ref, ref, sem).wait()


def columns_of(row):
    n = row.shape[1]
    return jnp.broadcast_to(row, (n, n)).T


def slot_targets(rows, cols, cap, axis):
    n = rows[0].shape[1]
    here = lax.broadcasted_iota(jnp.int32, (n, n), 1 - axis)
    there = lax.broadcasted_iota(jnp.int32, (n, n), axis)
    targets = []
    for k in range(2):
        mine, others = (rows, cols) if axis == 0 else (cols, rows)
        count = None
        for other in range(2):
            before = there <= here if other < k else there < here
            hit = (others[other] == mine[k]) & before
            seen = jnp.sum(jnp.where(hit, 1.0, 0.0), axis=axis, keepdims=True)
            count = seen if count is None else count + seen
        own = mine[k] if axis == 0 else mine[k][:, 0:1]
        targets.append(own * cap + count)
    return targets


PIECES = 2
RS_PIECES = 2


def layer_kernel(
    nx, nz, cap,
    ids_ref, w_row_ref, tok_ref, cot_ref, wg_hbm, wu_hbm, wd_hbm,
    routed_ref, rcot_ref, mixed_ref, gtok_ref, groute_ref, gg_ref, gu_ref, gd_ref,
    wg_ref, wu_ref, wd_ref, sel_ref, tokbuf, slots, cslots, gu_acc, dh_acc, hid_ref, dgu_ref, w_col_ref,
    pick, hid_t, dgu_t, ret, rs0, rs, bk, islots, gret, mixb, rs2_0, rs2, dsrc, dret, dpart, dsum,
    routed_v, rcot_v, ggu_v, gd_v,
    ring_send, ring_recv, tpush_send, tpush_recv, tself_sem, cpush_send, cpush_recv, cself_sem,
    cring_send, cring_recv, weight_sem,
    push_send, push_recv, self_sem, rs_send, rs_recv, g_send, g_recv, rs2_send, rs2_recv,
    d_send, d_recv, z_send, z_recv, load_sem, store_sem,
):
    me, t = lax.axis_index("expert"), lax.axis_index("tensor")
    n_tok, width = tok_ref.shape
    rows, h = hid_ref.shape
    half, thalf = rows // 2, n_tok // 2
    right, left = lax.rem(t + 1, nz), lax.rem(t + nz - 1, nz)
    tile = 128
    barrier = pltpu.get_barrier_semaphore()

    def hello(i, _):
        pl.semaphore_signal(
            barrier, inc=1, device_id={"expert": lax.rem(me + i, nx), "tensor": t}, device_id_type=MESH
        )
        return 0

    def hello_z(i, _):
        pl.semaphore_signal(
            barrier, inc=1, device_id={"expert": me, "tensor": lax.rem(t + i, nz)}, device_id_type=MESH
        )
        return 0

    lax.fori_loop(1, nx, hello, 0)
    lax.fori_loop(1, nz, hello_z, 0)
    weight_loads = [
        pltpu.make_async_copy(src, dst, weight_sem.at[i])
        for i, (src, dst) in enumerate(((wg_hbm, wg_ref), (wu_hbm, wu_ref), (wd_hbm, wd_ref)))
    ]
    for c in weight_loads:
        c.start()

    def slab(e):
        return pl.ds(pl.multiple_of(e * cap, cap), cap)

    def at(step):
        return lax.rem(t + 2 * nz + step, nz)

    order = [-1, 1]
    for j in range(2, nz // 2):
        order += [-j, j]
    order += [nz // 2, 0]
    started = []

    def go(c):
        c.start()
        started.append(c)

    id_rows = [ids_ref[k : k + 1, :].astype(F32) for k in range(2)]
    id_cols = [columns_of(r) for r in id_rows]
    row_targets = slot_targets(id_rows, id_cols, cap, 0)
    w0, w1 = w_row_ref[0:1, :], w_row_ref[1:2, :]
    for k in range(2):
        w_col_ref[:, k : k + 1] = columns_of(w_row_ref[k : k + 1, :])[:, 0:1]

    def select(i, _):
        r = pl.ds(pl.multiple_of(i * tile, tile), tile)
        j = (lax.broadcasted_iota(jnp.int32, (tile, n_tok), 0) + i * tile).astype(F32)
        hit0, hit1 = j == row_targets[0], j == row_targets[1]
        sel = jnp.where(hit0 | hit1, 1.0, 0.0).astype(BF16)
        sel_ref[r, :] = sel
        w = jnp.sum(jnp.where(hit0, w0, 0.0) + jnp.where(hit1, w1, 0.0), axis=1, keepdims=True)
        cslots[r, :] = (w * jnp.dot(sel, cot_ref[...], preferred_element_type=F32)).astype(BF16)
        return 0

    lax.fori_loop(0, rows // tile, select, 0)

    def fill(o, block):
        def body(i, _):
            r = pl.ds(pl.multiple_of(i * tile, tile), tile)
            slots[o, r, :] = jnp.dot(sel_ref[r, :], block[...], preferred_element_type=F32).astype(BF16)
            return 0

        lax.fori_loop(0, rows // tile, body, 0)

    pl.semaphore_wait(barrier, nx + nz - 2)

    def ring(d, k):
        o = at((-k, k)[d])
        return remote(
            tok_ref if k == 0 else tokbuf.at[o], tokbuf.at[o], ring_send.at[d, k], ring_recv.at[d, k],
            expert=me, tensor=(right, left)[d],
        )

    ring_hops = (nz // 2, nz - 1 - nz // 2)
    go(ring(0, 0))
    go(ring(1, 0))

    def push_cot(i, _):
        q = lax.rem(me + i, nx)
        remote(cslots.at[slab(q)], rcot_ref.at[t, slab(me)], cpush_send, cpush_recv, expert=q, tensor=t).start()
        return 0

    lax.fori_loop(1, nx, push_cot, 0)
    own_cot = pltpu.make_async_copy(cslots.at[slab(me)], rcot_ref.at[t, slab(me)], cself_sem)
    own_cot.start()
    token_order, token_owns = [], []

    def push_tok(step):
        i, o = len(token_order), at(step)

        def body(j, _):
            q = lax.rem(me + j, nx)
            remote(
                slots.at[o, slab(q)], routed_ref.at[o, slab(me)], tpush_send.at[i], tpush_recv.at[i],
                expert=q, tensor=t,
            ).start()
            return 0

        lax.fori_loop(1, nx, body, 0)
        own = pltpu.make_async_copy(slots.at[o, slab(me)], routed_ref.at[o, slab(me)], tself_sem.at[i])
        own.start()
        token_owns.append(own)
        token_order.append(step)

    def cot_ring(d, k, p):
        o, size = at((-k, k)[d]), half // PIECES
        r = pl.ds(d * half + p * size, size)
        return remote(
            rcot_ref.at[o, r], rcot_ref.at[o, r], cring_send.at[d, k, p], cring_recv.at[d, k, p],
            expert=me, tensor=(right, left)[d],
        )

    def token_step(k):
        came = [d for d in range(2) if k <= ring_hops[d]]
        for d in came:
            ring(d, k - 1).wait_recv()
            if k < ring_hops[d]:
                go(ring(d, k))
        for d in came:
            step = (-k, k)[d]
            fill(at(step), tokbuf.at[at(step)])
            push_tok(step)

    def cot_step(k):
        for p in range(PIECES):
            for d in range(2):
                if k > 0:
                    cot_ring(d, k - 1, p).wait_recv()
                if k < nz - 1:
                    go(cot_ring(d, k, p))

    def half_load(d, k):
        r = pl.ds(d * half, half)
        return pltpu.make_async_copy(
            rcot_ref.at[at((-k, k)[d]), r], rcot_v.at[k % 2, r], load_sem.at[d, k % 2]
        )

    def start_cot(k):
        for d in range(2):
            half_load(d, k).start()

    def add_cot(k):
        for d in range(2):
            r = pl.ds(d * half, half)
            half_load(d, k).wait()
            cols = pl.ds(pl.multiple_of(at((-k, k)[d]) * width, 128), width)
            dh = lax.dot_general(rcot_v[k % 2, r, :], wd_ref[:, cols], NT_DIMS, preferred_element_type=F32)
            dh_acc[r, :] = dh if k == 0 else dh_acc[r, :] + dh

    def tok_load(i):
        return pltpu.make_async_copy(routed_ref.at[at(token_order[i])], routed_v.at[i % 2], tself_sem.at[i])

    def start_tok(i):
        token_owns[i].wait()
        wait_bytes(slots.at[0, pl.ds(0, rows - cap)], tpush_recv.at[i])
        tok_load(i).start()

    def add_tok(i):
        tok_load(i).wait()
        w = weight_block(at(token_order[i]))
        for j in range(rows // tile):
            r = pl.ds(j * tile, tile)
            gu = jnp.dot(routed_v[i % 2, r, :], w, preferred_element_type=F32)
            gu_acc[r, :] = gu if i == 0 else gu_acc[r, :] + gu

    def weight_block(o):
        r = pl.ds(pl.multiple_of(o * width, 128), width)
        return jnp.concatenate([wg_ref[r, :], wu_ref[r, :]], axis=1)

    def fill_bk(d, o, into):
        w = weight_block(o)
        for i in range(half // tile):
            lhs = dgu_ref[pl.ds(d * half + i * tile, tile), :]
            into[d, pl.ds(i * tile, tile), :] = lax.dot_general(
                lhs, w, NT_DIMS, preferred_element_type=F32
            ).astype(into.dtype)

    def rs_copy(k, d, p):
        size = half // RS_PIECES
        r = pl.ds(p * size, size)
        return remote(
            rs0.at[d, r] if k == 0 else rs.at[d, k - 1, r], rs.at[d, k, r],
            rs_send.at[d, k, p], rs_recv.at[d, k, p], expert=me, tensor=(right, left)[d],
        )

    fill(t, tok_ref)
    push_tok(0)
    token_step(1)
    wait_bytes(cslots.at[pl.ds(0, rows - cap)], cpush_recv)
    own_cot.wait()
    cot_step(0)
    start_cot(0)
    token_step(2)
    cot_step(1)
    for c in weight_loads:
        c.wait()
    add_cot(0)
    start_cot(1)
    token_step(3)
    cot_step(2)
    add_cot(1)
    start_cot(2)
    token_step(4)
    cot_step(3)
    start_tok(0)
    add_cot(2)
    start_cot(3)
    add_tok(0)
    cot_step(4)
    start_tok(1)
    add_cot(3)
    start_cot(4)
    add_tok(1)
    cot_step(5)
    start_tok(2)
    add_cot(4)
    start_cot(5)
    add_tok(2)
    cot_step(6)
    start_tok(3)
    add_cot(5)
    start_cot(6)
    add_tok(3)
    start_tok(4)
    add_cot(6)
    cot_step(7)
    start_cot(7)
    add_tok(4)
    start_tok(5)
    add_cot(7)
    add_tok(5)
    start_tok(6)
    add_tok(6)
    lanes = lax.broadcasted_iota(jnp.int32, (n_tok, rows), 1).astype(F32)
    for k, target in enumerate(slot_targets(id_rows, id_cols, cap, 1)):
        pick[pl.ds(k * n_tok, n_tok), :] = jnp.where(lanes == target, 1.0, 0.0).astype(BF16)
    start_tok(7)
    add_tok(7)
    for i in range(nz):
        wait_bytes(slots.at[0, pl.ds(0, rows - cap)], tpush_send.at[i])

    for j in range(rows // tile):
        r = pl.ds(j * tile, tile)
        gate, up, d_hidden = gu_acc[r, :h], gu_acc[r, h:], dh_acc[r, :]
        sig = 1.0 / (1.0 + jnp.exp(-gate))
        silu = gate * sig
        hidden = (silu * up).astype(BF16)
        hid_ref[r, :] = hidden
        dgu_ref[r, :h] = (d_hidden * up * sig * (1.0 + gate * (1.0 - sig))).astype(BF16)
        dgu_ref[r, h:] = (d_hidden * silu).astype(BF16)
        dots = jnp.sum(hidden.astype(F32) * d_hidden, axis=1, keepdims=True)
        dsrc[r, :] = jnp.broadcast_to(dots, (tile, dsrc.shape[1]))


    def push_dots(i, _):
        q = lax.rem(me + i, nx)
        remote(dsrc.at[slab(q)], dret.at[slab(me)], d_send, d_recv, expert=q, tensor=t).start()
        return 0

    owns = []

    def down(i):
        o = at(order[i])
        cols = pl.ds(pl.multiple_of(o * width, 128), width)

        def body(j, _):
            r = pl.ds(pl.multiple_of(j * tile, tile), tile)
            slots[o, r, :] = jnp.dot(hid_ref[r, :], wd_ref[:, cols], preferred_element_type=F32).astype(BF16)
            return 0

        lax.fori_loop(0, rows // tile, body, 0)

        def push(j, _):
            q = lax.rem(me + j, nx)
            remote(
                slots.at[o, slab(q)], ret.at[o, slab(me)], push_send.at[i], push_recv.at[i], expert=q, tensor=t
            ).start()
            return 0

        lax.fori_loop(1, nx, push, 0)
        own = pltpu.make_async_copy(slots.at[o, slab(me)], ret.at[o, slab(me)], self_sem.at[i])
        own.start()
        owns.append(own)

    down(0)
    fill_bk(0, at(-1), rs0)
    fill_bk(1, at(1), rs0)
    for p in range(RS_PIECES):
        for d in range(2):
            go(rs_copy(0, d, p))
    lax.fori_loop(1, nx, push_dots, 0)
    dret[slab(me), :] = dsrc[slab(me), :]
    down(1)

    hid_t[...] = hid_ref[...].astype(F32).T.astype(BF16)
    dgu_t[...] = dgu_ref[...].astype(F32).T.astype(BF16)

    def load(o):
        return (
            pltpu.make_async_copy(routed_ref.at[o], routed_v.at[o % 2], load_sem.at[0, o % 2]),
            pltpu.make_async_copy(rcot_ref.at[o], rcot_v.at[o % 2], load_sem.at[1, o % 2]),
        )

    def store(o):
        r = pl.ds(o * width, width)
        return (
            pltpu.make_async_copy(ggu_v.at[o % 2, 0], gg_ref.at[r], store_sem.at[0, o % 2]),
            pltpu.make_async_copy(ggu_v.at[o % 2, 1], gu_ref.at[r], store_sem.at[1, o % 2]),
            pltpu.make_async_copy(gd_v.at[o % 2], gd_ref.at[:, r], store_sem.at[2, o % 2]),
        )

    for c in load(0):
        c.start()

    def grads(o):
        for c in load(o):
            c.wait()
        if o + 1 < nz:
            for c in load(o + 1):
                c.start()
        if o >= 2:
            for c in store(o - 2):
                c.wait()
        s = o % 2
        gd_v[s] = jnp.dot(hid_t[...], rcot_v[s], preferred_element_type=F32).astype(BF16)
        both = jnp.dot(dgu_t[...], routed_v[s], preferred_element_type=F32).T.astype(BF16)
        ggu_v[s, 0] = both[:, :h]
        ggu_v[s, 1] = both[:, h:]
        for c in store(o):
            c.start()

    def mix(i):
        o = at(order[i])
        owns[i].wait()
        wait_bytes(ret.at[0, pl.ds(0, rows - cap)], push_recv.at[i])
        chosen = jnp.dot(pick[...], ret[o], preferred_element_type=F32)
        mixb[o] = w_col_ref[:, 0:1] * chosen[:n_tok] + w_col_ref[:, 1:2] * chosen[n_tok:]

    def rs2_copy(k, d):
        return remote(
            rs2_0.at[d] if k == 0 else rs2.at[d, k - 1], rs2.at[d, k],
            rs2_send.at[d, k], rs2_recv.at[d, k], expert=me, tensor=(right, left)[d],
        )

    def rs2_step(k):
        for d in range(2):
            o = at((-1 - k, 1 + k)[d])
            part = mixb[o, pl.ds(d * thalf, thalf), :]
            if k == 0:
                rs2_0[d] = part.astype(BF16)
            else:
                rs2_copy(k - 1, d).wait_recv()
                part = rs2[d, k - 1].astype(F32) + part
                if k < nz - 1:
                    rs2[d, k - 1] = part.astype(BF16)
                else:
                    mixed_ref[pl.ds(d * thalf, thalf), :] = part.astype(BF16)
            if k < nz - 1:
                go(rs2_copy(k, d))

    def route_part():
        wait_bytes(dret.at[pl.ds(0, rows - cap)], d_recv)
        j = lax.broadcasted_iota(jnp.int32, (rows, n_tok), 0).astype(F32)
        dpart[...] = jnp.zeros_like(dpart)
        for k, target in enumerate(row_targets):
            dpart[k : k + 1, :] = jnp.sum(jnp.where(j == target, dret[...], 0.0), axis=0, keepdims=True)

        def share(i, _):
            remote(dpart, dsum.at[t], z_send, z_recv, expert=me, tensor=lax.rem(t + i, nz)).start()
            return 0

        lax.fori_loop(1, nz, share, 0)
        dsum[t] = dpart[...]

    size = half // RS_PIECES
    for k in range(1, nz):
        for d in range(2):
            fill_bk(d, at((-1 - k, 1 + k)[d]), bk)
        if k + 1 < nz:
            down(k + 1)
        for p in range(RS_PIECES):
            r = pl.ds(p * size, size)
            for d in range(2):
                rs_copy(k - 1, d, p).wait_recv()
                total = (rs[d, k - 1, r, :].astype(F32) + bk[d, r, :]).astype(BF16)
                if k < nz - 1:
                    rs[d, k - 1, r, :] = total
                    go(rs_copy(k, d, p))
                    continue
                islots[pl.ds(d * half + p * size, size), :] = total
                first, count = (d * half + p * size) // cap, size // cap

                def push_grad(i, _):
                    q = first + lax.rem(me + i, count)

                    @pl.when(q != me)
                    def _():
                        remote(islots.at[slab(q)], gret.at[slab(me)], g_send, g_recv, expert=q, tensor=t).start()

                    return 0

                lax.fori_loop(0, count, push_grad, 0)
        grads(k - 1)
        if k >= 2:
            mix(k - 2)
        if k == 2:
            route_part()
        if k in (3, 5, 7):
            rs2_step((k - 3) // 2)
    gret[slab(me), :] = islots[slab(me), :]
    grads(nz - 1)
    mix(nz - 2)
    for k in range(3, nz - 1):
        rs2_step(k)
    mix(nz - 1)
    wait_bytes(gret.at[pl.ds(0, rows - cap)], g_recv)
    chosen = jnp.dot(pick[...], gret[...], preferred_element_type=F32)
    gtok_ref[...] = (w_col_ref[:, 0:1] * chosen[:n_tok] + w_col_ref[:, 1:2] * chosen[n_tok:]).astype(BF16)
    rs2_step(nz - 1)

    wait_bytes(dsum.at[pl.ds(0, nz - 1)], z_recv)
    total = dsum[0]
    for z in range(1, nz):
        total = total + dsum[z]
    groute_ref[...] = total[0:2, :] / w_row_ref[...]

    for o in (nz - 2, nz - 1):
        for c in store(o):
            c.wait()
    for c in started:
        c.wait_send()
    for i in range(nz):
        wait_bytes(slots.at[0, pl.ds(0, rows - cap)], push_send.at[i])
    wait_bytes(islots.at[pl.ds(0, rows - cap)], g_send)
    wait_bytes(dsrc.at[pl.ds(0, rows - cap)], d_send)
    wait_bytes(dsum.at[pl.ds(0, nz - 1)], z_send)
    wait_bytes(cslots.at[pl.ds(0, rows - cap)], cpush_send)


def layer(nx, nz, cap, ids_t, weights_t, tokens, cotangent, wg, wu, wd):
    n_tok, width = tokens.shape
    h = wg.shape[1]
    rows = nx * cap
    dma = pltpu.SemaphoreType.DMA
    small = jax.ShapeDtypeStruct((n_tok, width), BF16)
    tall = jax.ShapeDtypeStruct((nz * width, h), BF16)
    buffer = jax.ShapeDtypeStruct((nz, rows, width), BF16)
    return pl.pallas_call(
        functools.partial(layer_kernel, nx, nz, cap),
        out_shape=(
            buffer, buffer, small, small, jax.ShapeDtypeStruct((2, n_tok), F32), tall, tall,
            jax.ShapeDtypeStruct((h, nz * width), BF16),
        ),
        in_specs=[VMEM] * 4 + [ANY] * 3,
        out_specs=(ANY, ANY, VMEM, VMEM, VMEM, ANY, ANY, ANY),
        scratch_shapes=[
            pltpu.VMEM((nz * width, h), BF16),
            pltpu.VMEM((nz * width, h), BF16),
            pltpu.VMEM((h, nz * width), BF16),
            pltpu.VMEM((rows, n_tok), BF16),
            pltpu.VMEM((nz, n_tok, width), BF16),
            pltpu.VMEM((nz, rows, width), BF16),
            pltpu.VMEM((rows, width), BF16),
            pltpu.VMEM((rows, 2 * h), F32),
            pltpu.VMEM((rows, h), F32),
            pltpu.VMEM((rows, h), BF16),
            pltpu.VMEM((rows, 2 * h), BF16),
            pltpu.VMEM((n_tok, 2), F32),
            pltpu.VMEM((2 * n_tok, rows), BF16),
            pltpu.VMEM((h, rows), BF16),
            pltpu.VMEM((2 * h, rows), BF16),
            pltpu.VMEM((nz, rows, width), BF16),
            pltpu.VMEM((2, rows // 2, width), BF16),
            pltpu.VMEM((2, nz - 1, rows // 2, width), BF16),
            pltpu.VMEM((2, rows // 2, width), F32),
            pltpu.VMEM((rows, width), BF16),
            pltpu.VMEM((rows, width), BF16),
            pltpu.VMEM((nz, n_tok, width), F32),
            pltpu.VMEM((2, n_tok // 2, width), BF16),
            pltpu.VMEM((2, nz - 1, n_tok // 2, width), BF16),
            pltpu.VMEM((rows, 128), F32),
            pltpu.VMEM((rows, 128), F32),
            pltpu.VMEM((8, n_tok), F32),
            pltpu.VMEM((nz, 8, n_tok), F32),
            pltpu.VMEM((2, rows, width), BF16),
            pltpu.VMEM((2, rows, width), BF16),
            pltpu.VMEM((2, 2, width, h), BF16),
            pltpu.VMEM((2, h, width), BF16),
            dma((2, nz // 2)), dma((2, nz // 2)), dma((nz,)), dma((nz,)), dma((nz,)), dma, dma, dma,
            dma((2, nz - 1, PIECES)), dma((2, nz - 1, PIECES)), dma((3,)),
            dma((nz,)), dma((nz,)), dma((nz,)),
            dma((2, nz - 1, RS_PIECES)), dma((2, nz - 1, RS_PIECES)),
            dma, dma, dma((2, nz - 1)), dma((2, nz - 1)),
            dma, dma, dma, dma, dma((2, 2)), dma((3, 2)),
        ],
        compiler_params=pltpu.CompilerParams(
            collective_id=0, has_side_effects=True, vmem_limit_bytes=62 * 1024 * 1024
        ),
        name="layer",
    )(ids_t, weights_t, tokens, cotangent, wg, wu, wd)


def local(tokens, ids, weights, cotangent, w_gate, w_up, w_down):
    nx, nz = lax.axis_size("expert"), lax.axis_size("tensor")
    cap = 4 * tokens.shape[0] // nx
    _, _, mixed, grad_tokens, grad_route, grad_gate, grad_up, grad_down = layer(
        nx, nz, cap, ids.T, weights.T, tokens, cotangent, w_gate[0], w_up[0], w_down[0]
    )
    return (mixed, grad_tokens, grad_route.T, grad_gate[None], grad_up[None], grad_down[None])


def solution(mesh):
    placed = (
        P("expert", "tensor"),
        P("expert", None),
        P("expert", None),
        P("expert", "tensor"),
        P("expert", None, "tensor"),
        P("expert", None, "tensor"),
        P("expert", "tensor", None),
    )
    return jax.shard_map(
        local,
        mesh=mesh,
        in_specs=placed,
        out_specs=(
            P("expert", "tensor"),
            P("expert", "tensor"),
            P("expert", None),
            P("expert", None, "tensor"),
            P("expert", None, "tensor"),
            P("expert", "tensor", None),
        ),
        check_vma=False,
    )
```

time: 531 us -> 236 us (0.44); the launches traced: 523 us -> 234 us
  waiting for transfers between devices: 296 us -> 0 us
  Pallas kernels: 0 us -> 222 us
  local copies, waits for them, and re-layouts: 75.8 us -> 10.9 us
  matrix products: 60 us -> 0 us
  starting transfers between devices: 33 us -> 0 us
  blocking collectives: 28.7 us -> 0 us
  other arithmetic: 15.6 us -> 0 us
  between operations: 14.2 us -> 0.65 us
    pallas_call x0 -> x1, Pallas kernels: none -> 222 us  [layer(): pl.pallas_call(functools.partial(layer_kernel, nx, nz, cap), out_shape=(b...]
    unnamed x6 -> x0, waiting for transfers between devices: 122 us -> none
    all_to_all x4 -> x0, waiting for transfers between devices: 95.9 us -> none  [the longest x1 76.3 us: local(): lax.all_to_all(cot_slots.reshape(experts, capacity, model_width), 'expert...]
    all_gather x2 -> x0, waiting for transfers between devices: 77.8 us -> none  [the longest x1 40.9 us: local(): lax.all_gather(tokens, 'tensor', axis=1, tiled=True)]
    dot_general x9 -> x0, matrix products: 60 us -> none  [the longest x1 10.9 us: local(): lax.dot_general(up_gradient, up_matrix, ROW_PAIRS, preferred_element_type...]
    gather x5 -> x0, local copies, waits for them, and re-layouts: 38.6 us -> none  [the longest x1 15.6 us: fill_slots(): token_slots = padded_tokens[row_of]]
    all_to_all x4 -> x0, starting transfers between devices: 32.2 us -> none  [the longest x1 9.41 us: local(): lax.all_to_all(cot_slots.reshape(experts, capacity, model_width), 'expert...]
    psum x1 -> x0, blocking collectives: 28.7 us -> none  [local(): grad_route = lax.psum(route_part, 'tensor')]
  transfers between devices with their start and end apart: 8 -> 0, of which waited for: 7 -> 0; matrix products, arithmetic and copies ran while one was open for 20% -> 0% of each run, Pallas kernels for 0% -> 0%
where the time goes in v2:
time: 236 us; the launch traced here: 234 us
  Pallas kernels  222 us (94%)
  local copies, waits for them, and re-layouts  10.9 us (5%)
    pallas_call x1, Pallas kernels, layer(): pl.pallas_call(functools.partial(layer_kernel, nx, nz, cap), out_shape=(b...  222 us
    unnamed x10, local copies, waits for them, and re-layouts  10.9 us

profile of v2, /device:TPU:2, one launch (start us, length us, event | category | flops | bytes accessed | tf_op | source)
XLA Modules:
  0.0 233.9 jit_solution(13545993144519203315)
XLA Ops:
  0.6 222.3 %layer.1 = (bf16[8,512,896]{2,1,0:T(8,128)(2,1)}, bf16[8,512,896]{2,1,0:T(8,128)(2,1)}, bf16[128,896]{1,0:T(8,128)(2,1)}, bf16[128,896]{1,0:T(8,128)(2,1)}, f32[...) custom-call(s32[2,128]{1,0:T(2,128)} %bitcast.16, ...), custom_call_target="tpu_custom_call" | custom-call | tf_op jit(solution)/shard_map/layer/pallas_call | solution.py:522
  222.9 1.6 copy.19
  224.6 1.6 copy.20
  226.2 1.2 copy.21
  227.5 0.0 copy-start.1
  227.5 3.0 %copy.22 = bf16[1,7168,128]{2,1,0:T(8,128)(2,1)} copy(bf16[1,7168,128]{2,1,0:T(8,128)(2,1)} %bitcast.11) | data formatting | bytes 3670016
  230.5 0.0 copy-done.1
  230.5 0.0 copy-start
  230.5 1.2 copy.23
  231.7 0.9 copy-done
  232.6 1.2 copy.24
Async XLA Ops:
  227.5 3.0 %copy-start.1 = (bf16[7168,128]{1,0:T(8,128)(2,1)S(1)}, bf16[7168,128]{1,0:T(8,128)(2,1)}, u32[]{:S(2)}) copy-start(bf16[7168,128]{1,0:T(8,128)(2,1)} %get-tuple-element.16) | copy-start | bytes 5505028
  230.5 2.2 copy-start

commit v3 on v2

--- a/solution.py
+++ b/solution.py
@@ -50,6 +50,7 @@
 
 PIECES = 2
 RS_PIECES = 2
+RS2_LAG = 4
 
 
 def layer_kernel(
@@ -57,10 +58,10 @@
     ids_ref, w_row_ref, tok_ref, cot_ref, wg_hbm, wu_hbm, wd_hbm,
     routed_ref, rcot_ref, mixed_ref, gtok_ref, groute_ref, gg_ref, gu_ref, gd_ref,
     wg_ref, wu_ref, wd_ref, sel_ref, tokbuf, slots, cslots, gu_acc, dh_acc, hid_ref, dgu_ref, w_col_ref,
-    pick, hid_t, dgu_t, ret, rs0, rs, bk, islots, gret, mixb, rs2_0, rs2, dsrc, dret, dpart, dsum,
+    pick, hid_t, dgu_t, ret, rs0, rs, bk, islots, gret, mix_v, rs2_0, rs2, dsrc, dret, dpart, dsum,
     routed_v, rcot_v, ggu_v, gd_v,
     ring_send, ring_recv, tpush_send, tpush_recv, tself_sem, cpush_send, cpush_recv, cself_sem,
-    cring_send, cring_recv, weight_sem,
+    cring_send, cring_recv, cload_sem, weight_sem,
     push_send, push_recv, self_sem, rs_send, rs_recv, g_send, g_recv, rs2_send, rs2_recv,
     d_send, d_recv, z_send, z_recv, load_sem, store_sem,
 ):
@@ -99,10 +100,6 @@
     def at(step):
         return lax.rem(t + 2 * nz + step, nz)
 
-    order = [-1, 1]
-    for j in range(2, nz // 2):
-        order += [-j, j]
-    order += [nz // 2, 0]
     started = []
 
     def go(c):
@@ -136,18 +133,21 @@
 
         lax.fori_loop(0, rows // tile, body, 0)
 
+    fill(t, tok_ref)
     pl.semaphore_wait(barrier, nx + nz - 2)
 
-    def ring(d, k):
-        o = at((-k, k)[d])
+    def ring(d, k, p):
+        o, size = at((-k, k)[d]), n_tok // PIECES
+        r = pl.ds(p * size, size)
         return remote(
-            tok_ref if k == 0 else tokbuf.at[o], tokbuf.at[o], ring_send.at[d, k], ring_recv.at[d, k],
-            expert=me, tensor=(right, left)[d],
+            tok_ref.at[r] if k == 0 else tokbuf.at[o, r], tokbuf.at[o, r],
+            ring_send.at[d, k, p], ring_recv.at[d, k, p], expert=me, tensor=(right, left)[d],
         )
 
     ring_hops = (nz // 2, nz - 1 - nz // 2)
-    go(ring(0, 0))
-    go(ring(1, 0))
+    for p in range(PIECES):
+        for d in range(2):
+            go(ring(d, 0, p))
 
     def push_cot(i, _):
         q = lax.rem(me + i, nx)
@@ -186,14 +186,22 @@
 
     def token_step(k):
         came = [d for d in range(2) if k <= ring_hops[d]]
-        for d in came:
-            ring(d, k - 1).wait_recv()
-            if k < ring_hops[d]:
-                go(ring(d, k))
+        for p in range(PIECES):
+            for d in came:
+                ring(d, k - 1, p).wait_recv()
+                if k < ring_hops[d]:
+                    go(ring(d, k, p))
         for d in came:
             step = (-k, k)[d]
             fill(at(step), tokbuf.at[at(step)])
             push_tok(step)
+
+    def cot_load(d, k, p):
+        size = half // PIECES
+        r = pl.ds(d * half + p * size, size)
+        return pltpu.make_async_copy(
+            rcot_ref.at[at((-k, k)[d]), r], rcot_v.at[k % 2, r], cload_sem.at[d, k % 2, p]
+        )
 
     def cot_step(k):
         for p in range(PIECES):
@@ -202,21 +210,13 @@
                     cot_ring(d, k - 1, p).wait_recv()
                 if k < nz - 1:
                     go(cot_ring(d, k, p))
-
-    def half_load(d, k):
-        r = pl.ds(d * half, half)
-        return pltpu.make_async_copy(
-            rcot_ref.at[at((-k, k)[d]), r], rcot_v.at[k % 2, r], load_sem.at[d, k % 2]
-        )
-
-    def start_cot(k):
-        for d in range(2):
-            half_load(d, k).start()
+                cot_load(d, k, p).start()
 
     def add_cot(k):
         for d in range(2):
             r = pl.ds(d * half, half)
-            half_load(d, k).wait()
+            for p in range(PIECES):
+                cot_load(d, k, p).wait()
             cols = pl.ds(pl.multiple_of(at((-k, k)[d]) * width, 128), width)
             dh = lax.dot_general(rcot_v[k % 2, r, :], wd_ref[:, cols], NT_DIMS, preferred_element_type=F32)
             dh_acc[r, :] = dh if k == 0 else dh_acc[r, :] + dh
@@ -257,115 +257,117 @@
             rs_send.at[d, k, p], rs_recv.at[d, k, p], expert=me, tensor=(right, left)[d],
         )
 
-    fill(t, tok_ref)
     push_tok(0)
     token_step(1)
     wait_bytes(cslots.at[pl.ds(0, rows - cap)], cpush_recv)
     own_cot.wait()
     cot_step(0)
-    start_cot(0)
     token_step(2)
     cot_step(1)
     for c in weight_loads:
         c.wait()
     add_cot(0)
-    start_cot(1)
     token_step(3)
     cot_step(2)
     add_cot(1)
-    start_cot(2)
     token_step(4)
     cot_step(3)
     start_tok(0)
     add_cot(2)
-    start_cot(3)
+    start_tok(1)
     add_tok(0)
     cot_step(4)
-    start_tok(1)
+    start_tok(2)
     add_cot(3)
-    start_cot(4)
     add_tok(1)
+    start_tok(3)
+    add_tok(2)
     cot_step(5)
-    start_tok(2)
+    start_tok(4)
     add_cot(4)
-    start_cot(5)
-    add_tok(2)
+    add_tok(3)
+    start_tok(5)
+    add_tok(4)
     cot_step(6)
-    start_tok(3)
+    start_tok(6)
     add_cot(5)
-    start_cot(6)
-    add_tok(3)
-    start_tok(4)
+    add_tok(5)
+    add_tok(6)
     add_cot(6)
-    cot_step(7)
-    start_cot(7)
-    add_tok(4)
-    start_tok(5)
-    add_cot(7)
-    add_tok(5)
-    start_tok(6)
-    add_tok(6)
     lanes = lax.broadcasted_iota(jnp.int32, (n_tok, rows), 1).astype(F32)
     for k, target in enumerate(slot_targets(id_rows, id_cols, cap, 1)):
         pick[pl.ds(k * n_tok, n_tok), :] = jnp.where(lanes == target, 1.0, 0.0).astype(BF16)
     start_tok(7)
     add_tok(7)
+
+    def gates(r):
+        gate, up = gu_acc[r, :h], gu_acc[r, h:]
+        sig = 1.0 / (1.0 + jnp.exp(-gate))
+        return gate, up, sig, gate * sig
+
+    for j in range(rows // tile):
+        r = pl.ds(j * tile, tile)
+        gate, up, sig, silu = gates(r)
+        hid_ref[r, :] = (silu * up).astype(BF16)
     for i in range(nz):
         wait_bytes(slots.at[0, pl.ds(0, rows - cap)], tpush_send.at[i])
 
+    split = 128 * ((width // 128 + 1) // 2)
+    parts = ((0, split), (split, width - split))
+    owns = {}
+
+    def down(u, sides=(0, 1)):
+        for d in sides:
+            o = at((-1 - u, 1 + u)[d])
+            first, count = parts[d]
+            cols, here = pl.ds(pl.multiple_of(o * width + first, 128), count), pl.ds(first, count)
+
+            def body(j, _):
+                r = pl.ds(pl.multiple_of(j * tile, tile), tile)
+                slots[o, r, here] = jnp.dot(hid_ref[r, :], wd_ref[:, cols], preferred_element_type=F32).astype(BF16)
+                return 0
+
+            lax.fori_loop(0, rows // tile, body, 0)
+
+            def push(j, _):
+                q = lax.rem(me + j, nx)
+                remote(
+                    slots.at[o, slab(q), here], ret.at[o, slab(me), here],
+                    push_send.at[d, u], push_recv.at[d, u], expert=q, tensor=t,
+                ).start()
+                return 0
+
+            lax.fori_loop(1, nx, push, 0)
+            own = pltpu.make_async_copy(slots.at[o, slab(me), here], ret.at[o, slab(me), here], self_sem.at[d, u])
+            own.start()
+            owns[d, u] = own
+
+    down(0, (0,))
+    cot_step(7)
+    down(0, (1,))
+    add_cot(7)
     for j in range(rows // tile):
         r = pl.ds(j * tile, tile)
-        gate, up, d_hidden = gu_acc[r, :h], gu_acc[r, h:], dh_acc[r, :]
-        sig = 1.0 / (1.0 + jnp.exp(-gate))
-        silu = gate * sig
-        hidden = (silu * up).astype(BF16)
-        hid_ref[r, :] = hidden
+        gate, up, sig, silu = gates(r)
+        d_hidden = dh_acc[r, :]
         dgu_ref[r, :h] = (d_hidden * up * sig * (1.0 + gate * (1.0 - sig))).astype(BF16)
         dgu_ref[r, h:] = (d_hidden * silu).astype(BF16)
-        dots = jnp.sum(hidden.astype(F32) * d_hidden, axis=1, keepdims=True)
+        dots = jnp.sum(hid_ref[r, :].astype(F32) * d_hidden, axis=1, keepdims=True)
         dsrc[r, :] = jnp.broadcast_to(dots, (tile, dsrc.shape[1]))
-
 
     def push_dots(i, _):
         q = lax.rem(me + i, nx)
         remote(dsrc.at[slab(q)], dret.at[slab(me)], d_send, d_recv, expert=q, tensor=t).start()
         return 0
 
-    owns = []
-
-    def down(i):
-        o = at(order[i])
-        cols = pl.ds(pl.multiple_of(o * width, 128), width)
-
-        def body(j, _):
-            r = pl.ds(pl.multiple_of(j * tile, tile), tile)
-            slots[o, r, :] = jnp.dot(hid_ref[r, :], wd_ref[:, cols], preferred_element_type=F32).astype(BF16)
-            return 0
-
-        lax.fori_loop(0, rows // tile, body, 0)
-
-        def push(j, _):
-            q = lax.rem(me + j, nx)
-            remote(
-                slots.at[o, slab(q)], ret.at[o, slab(me)], push_send.at[i], push_recv.at[i], expert=q, tensor=t
-            ).start()
-            return 0
-
-        lax.fori_loop(1, nx, push, 0)
-        own = pltpu.make_async_copy(slots.at[o, slab(me)], ret.at[o, slab(me)], self_sem.at[i])
-        own.start()
-        owns.append(own)
-
-    down(0)
     fill_bk(0, at(-1), rs0)
     fill_bk(1, at(1), rs0)
     for p in range(RS_PIECES):
         for d in range(2):
             go(rs_copy(0, d, p))
+    down(1)
     lax.fori_loop(1, nx, push_dots, 0)
     dret[slab(me), :] = dsrc[slab(me), :]
-    down(1)
-
     hid_t[...] = hid_ref[...].astype(F32).T.astype(BF16)
     dgu_t[...] = dgu_ref[...].astype(F32).T.astype(BF16)
 
@@ -403,34 +405,34 @@
         for c in store(o):
             c.start()
 
-    def mix(i):
-        o = at(order[i])
-        owns[i].wait()
-        wait_bytes(ret.at[0, pl.ds(0, rows - cap)], push_recv.at[i])
-        chosen = jnp.dot(pick[...], ret[o], preferred_element_type=F32)
-        mixb[o] = w_col_ref[:, 0:1] * chosen[:n_tok] + w_col_ref[:, 1:2] * chosen[n_tok:]
-
     def rs2_copy(k, d):
+        cols = pl.ds(*parts[d])
         return remote(
-            rs2_0.at[d] if k == 0 else rs2.at[d, k - 1], rs2.at[d, k],
+            rs2_0.at[:, cols] if k == 0 else rs2.at[k - 1, :, cols], rs2.at[k, :, cols],
             rs2_send.at[d, k], rs2_recv.at[d, k], expert=me, tensor=(right, left)[d],
         )
 
-    def rs2_step(k):
+    def rs2_step(u):
         for d in range(2):
-            o = at((-1 - k, 1 + k)[d])
-            part = mixb[o, pl.ds(d * thalf, thalf), :]
-            if k == 0:
-                rs2_0[d] = part.astype(BF16)
+            o, cols = at((-1 - u, 1 + u)[d]), pl.ds(*parts[d])
+            owns[d, u].wait()
+            wait_bytes(ret.at[0, pl.ds(0, rows - cap), cols], push_recv.at[d, u])
+            chosen = jnp.dot(pick[...], ret[o, :, cols], preferred_element_type=F32)
+            mix_v[:, cols] = w_col_ref[:, 0:1] * chosen[:n_tok] + w_col_ref[:, 1:2] * chosen[n_tok:]
+        for d in range(2):
+            cols = pl.ds(*parts[d])
+            part = mix_v[:, cols]
+            if u == 0:
+                rs2_0[:, cols] = part.astype(BF16)
             else:
-                rs2_copy(k - 1, d).wait_recv()
-                part = rs2[d, k - 1].astype(F32) + part
-                if k < nz - 1:
-                    rs2[d, k - 1] = part.astype(BF16)
+                rs2_copy(u - 1, d).wait_recv()
+                part = rs2[u - 1, :, cols].astype(F32) + part
+                if u < nz - 1:
+                    rs2[u - 1, :, cols] = part.astype(BF16)
                 else:
-                    mixed_ref[pl.ds(d * thalf, thalf), :] = part.astype(BF16)
-            if k < nz - 1:
-                go(rs2_copy(k, d))
+                    mixed_ref[:, cols] = part.astype(BF16)
+            if u < nz - 1:
+                go(rs2_copy(u, d))
 
     def route_part():
         wait_bytes(dret.at[pl.ds(0, rows - cap)], d_recv)
@@ -475,18 +477,15 @@
 
                 lax.fori_loop(0, count, push_grad, 0)
         grads(k - 1)
-        if k >= 2:
-            mix(k - 2)
         if k == 2:
             route_part()
-        if k in (3, 5, 7):
-            rs2_step((k - 3) // 2)
+        if k >= RS2_LAG:
+            rs2_step(k - RS2_LAG)
     gret[slab(me), :] = islots[slab(me), :]
-    grads(nz - 1)
-    mix(nz - 2)
-    for k in range(3, nz - 1):
-        rs2_step(k)
-    mix(nz - 1)
+    for u in range(nz - RS2_LAG, nz - 1):
+        rs2_step(u)
+        if u == nz - RS2_LAG:
+            grads(nz - 1)
     wait_bytes(gret.at[pl.ds(0, rows - cap)], g_recv)
     chosen = jnp.dot(pick[...], gret[...], preferred_element_type=F32)
     gtok_ref[...] = (w_col_ref[:, 0:1] * chosen[:n_tok] + w_col_ref[:, 1:2] * chosen[n_tok:]).astype(BF16)
@@ -503,8 +502,9 @@
             c.wait()
     for c in started:
         c.wait_send()
-    for i in range(nz):
-        wait_bytes(slots.at[0, pl.ds(0, rows - cap)], push_send.at[i])
+    for d in range(2):
+        for u in range(nz):
+            wait_bytes(ret.at[0, pl.ds(0, rows - cap), pl.ds(*parts[d])], push_send.at[d, u])
     wait_bytes(islots.at[pl.ds(0, rows - cap)], g_send)
     wait_bytes(dsrc.at[pl.ds(0, rows - cap)], d_send)
     wait_bytes(dsum.at[pl.ds(0, nz - 1)], z_send)
@@ -549,9 +549,9 @@
             pltpu.VMEM((2, rows // 2, width), F32),
             pltpu.VMEM((rows, width), BF16),
             pltpu.VMEM((rows, width), BF16),
-            pltpu.VMEM((nz, n_tok, width), F32),
-            pltpu.VMEM((2, n_tok // 2, width), BF16),
-            pltpu.VMEM((2, nz - 1, n_tok // 2, width), BF16),
+            pltpu.VMEM((n_tok, width), F32),
+            pltpu.VMEM((n_tok, width), BF16),
+            pltpu.VMEM((nz - 1, n_tok, width), BF16),
             pltpu.VMEM((rows, 128), F32),
             pltpu.VMEM((rows, 128), F32),
             pltpu.VMEM((8, n_tok), F32),
@@ -560,9 +560,9 @@
             pltpu.VMEM((2, rows, width), BF16),
             pltpu.VMEM((2, 2, width, h), BF16),
             pltpu.VMEM((2, h, width), BF16),
-            dma((2, nz // 2)), dma((2, nz // 2)), dma((nz,)), dma((nz,)), dma((nz,)), dma, dma, dma,
-            dma((2, nz - 1, PIECES)), dma((2, nz - 1, PIECES)), dma((3,)),
-            dma((nz,)), dma((nz,)), dma((nz,)),
+            dma((2, nz // 2, PIECES)), dma((2, nz // 2, PIECES)), dma((nz,)), dma((nz,)), dma((nz,)), dma, dma, dma,
+            dma((2, nz - 1, PIECES)), dma((2, nz - 1, PIECES)), dma((2, 2, PIECES)), dma((3,)),
+            dma((2, nz)), dma((2, nz)), dma((2, nz)),
             dma((2, nz - 1, RS_PIECES)), dma((2, nz - 1, RS_PIECES)),
             dma, dma, dma((2, nz - 1)), dma((2, nz - 1)),
             dma, dma, dma, dma, dma((2, 2)), dma((3, 2)),
@@ -574,12 +574,56 @@
     )(ids_t, weights_t, tokens, cotangent, wg, wu, wd)
 
 
+CHUNKS = 4
+
+
+def finish_kernel(*refs):
+    n = 6
+    ins, outs, held, get, put = refs[:n], refs[n : 2 * n], refs[2 * n : 3 * n], refs[3 * n], refs[3 * n + 1]
+
+    def pieces():
+        at = 0
+        for a, (src, dst, v) in enumerate(zip(ins, outs, held)):
+            axis = 0 if src.shape[0] >= src.shape[1] else 1
+            size = src.shape[axis] // CHUNKS if max(src.shape) >= 1024 * CHUNKS else src.shape[axis]
+            for c in range(src.shape[axis] // size):
+                where = (pl.ds(c * size, size), slice(None)) if axis == 0 else (slice(None), pl.ds(c * size, size))
+                yield (
+                    pltpu.make_async_copy(src.at[where], v.at[where], get.at[at]),
+                    pltpu.make_async_copy(v.at[where], dst.at[where], put.at[at]),
+                )
+                at += 1
+
+    moves = list(pieces())
+    for load, _ in moves:
+        load.start()
+    for load, store in moves:
+        load.wait()
+        store.start()
+    for _, store in moves:
+        store.wait()
+
+
+def finish(*arrays):
+    n = len(arrays)
+    shapes = tuple(jax.ShapeDtypeStruct(a.shape, a.dtype) for a in arrays)
+    return pl.pallas_call(
+        finish_kernel,
+        out_shape=shapes,
+        in_specs=[ANY] * n,
+        out_specs=(ANY,) * n,
+        scratch_shapes=[pltpu.VMEM(a.shape, a.dtype) for a in arrays]
+        + [pltpu.SemaphoreType.DMA((n * CHUNKS,)), pltpu.SemaphoreType.DMA((n * CHUNKS,))],
+        compiler_params=pltpu.CompilerParams(vmem_limit_bytes=62 * 1024 * 1024),
+        name="finish",
+    )(*arrays)
+
+
 def local(tokens, ids, weights, cotangent, w_gate, w_up, w_down):
     nx, nz = lax.axis_size("expert"), lax.axis_size("tensor")
     cap = 4 * tokens.shape[0] // nx
-    _, _, mixed, grad_tokens, grad_route, grad_gate, grad_up, grad_down = layer(
-        nx, nz, cap, ids.T, weights.T, tokens, cotangent, w_gate[0], w_up[0], w_down[0]
-    )
+    results = layer(nx, nz, cap, ids.T, weights.T, tokens, cotangent, w_gate[0], w_up[0], w_down[0])
+    mixed, grad_tokens, grad_route, grad_gate, grad_up, grad_down = finish(*results[2:])
     return (mixed, grad_tokens, grad_route.T, grad_gate[None], grad_up[None], grad_down[None])
 
 

time: 236 us -> 218 us (0.924)
  local copies, waits for them, and re-layouts: 10.9 us -> 0 us
  Pallas kernels: 222 us -> 216 us
    pallas_call x1, Pallas kernels: 222 us -> 210 us  [layer(): pl.pallas_call(functools.partial(layer_kernel, nx, nz, cap), out_shape=(b...]
    unnamed x10 -> x0, local copies, waits for them, and re-layouts: 10.9 us -> none
    pallas_call x0 -> x1, Pallas kernels: none -> 5.46 us  [finish(): pl.pallas_call(finish_kernel, out_shape=shapes, in_specs=[ANY] * n, out_s...]
where the time goes in v3:
time: 218 us; the launch traced here: 217 us
  Pallas kernels  216 us (99%)
    pallas_call x1, Pallas kernels, layer(): pl.pallas_call(functools.partial(layer_kernel, nx, nz, cap), out_shape=(b...  210 us
    pallas_call x1, Pallas kernels, finish(): pl.pallas_call(finish_kernel, out_shape=shapes, in_specs=[ANY] * n, out_s...  5.46 us

profile of v3, /device:TPU:2, one launch (start us, length us, event | category | flops | bytes accessed | tf_op | source)
XLA Modules:
  0.0 216.8 jit_solution(13660994671962034343)
XLA Ops:
  0.6 210.5 %layer.1 = (bf16[8,512,896]{2,1,0:T(8,128)(2,1)}, bf16[8,512,896]{2,1,0:T(8,128)(2,1)}, bf16[128,896]{1,0:T(8,128)(2,1)}, bf16[128,896]{1,0:T(8,128)(2,1)}, f32[...) custom-call(s32[2,128]{1,0:T(2,128)} %bitcast.12, ...), custom_call_target="tpu_custom_call" | custom-call | tf_op jit(solution)/shard_map/layer/pallas_call | solution.py:522
  211.1 5.5 %finish.1 = (bf16[128,896]{1,0:T(8,128)(2,1)}, bf16[128,896]{1,0:T(8,128)(2,1)}, f32[2,128]{1,0:T(2,128)}, bf16[7168,128]{1,0:T(8,128)(2,1)}, bf16[7168,128]{1,0:T(8,128)(2,1)}, /*index=5*/bf16[128,7168]{1,0:T(8,128)(2,1)}) custom-call(bf16[128,896]{1,0:T(8,128)(2,1)} %get-tuple-element.18.refs_0_, bf16[128,896]{1,0:T(8,128)(2,1)} %get-tuple-element.19.refs_1_, ...), custom_call_target="tpu_custom_call" | custom-call | tf_op jit(solution)/shard_map/finish/pallas_call | solution.py:610

commit v4 on v3

--- a/solution.py
+++ b/solution.py
@@ -50,7 +50,7 @@
 
 PIECES = 2
 RS_PIECES = 2
-RS2_LAG = 4
+RS2_LAG = 3
 
 
 def layer_kernel(
@@ -59,11 +59,11 @@
     routed_ref, rcot_ref, mixed_ref, gtok_ref, groute_ref, gg_ref, gu_ref, gd_ref,
     wg_ref, wu_ref, wd_ref, sel_ref, tokbuf, slots, cslots, gu_acc, dh_acc, hid_ref, dgu_ref, w_col_ref,
     pick, hid_t, dgu_t, ret, rs0, rs, bk, islots, gret, mix_v, rs2_0, rs2, dsrc, dret, dpart, dsum,
-    routed_v, rcot_v, ggu_v, gd_v,
+    routed_v, rcot_v,
     ring_send, ring_recv, tpush_send, tpush_recv, tself_sem, cpush_send, cpush_recv, cself_sem,
     cring_send, cring_recv, cload_sem, weight_sem,
     push_send, push_recv, self_sem, rs_send, rs_recv, g_send, g_recv, rs2_send, rs2_recv,
-    d_send, d_recv, z_send, z_recv, load_sem, store_sem,
+    d_send, d_recv, z_send, z_recv, load_sem,
 ):
     me, t = lax.axis_index("expert"), lax.axis_index("tensor")
     n_tok, width = tok_ref.shape
@@ -377,14 +377,6 @@
             pltpu.make_async_copy(rcot_ref.at[o], rcot_v.at[o % 2], load_sem.at[1, o % 2]),
         )
 
-    def store(o):
-        r = pl.ds(o * width, width)
-        return (
-            pltpu.make_async_copy(ggu_v.at[o % 2, 0], gg_ref.at[r], store_sem.at[0, o % 2]),
-            pltpu.make_async_copy(ggu_v.at[o % 2, 1], gu_ref.at[r], store_sem.at[1, o % 2]),
-            pltpu.make_async_copy(gd_v.at[o % 2], gd_ref.at[:, r], store_sem.at[2, o % 2]),
-        )
-
     for c in load(0):
         c.start()
 
@@ -394,22 +386,19 @@
         if o + 1 < nz:
             for c in load(o + 1):
                 c.start()
-        if o >= 2:
-            for c in store(o - 2):
-                c.wait()
         s = o % 2
-        gd_v[s] = jnp.dot(hid_t[...], rcot_v[s], preferred_element_type=F32).astype(BF16)
+        r = pl.ds(o * width, width)
+        gd_ref[:, r] = jnp.dot(hid_t[...], rcot_v[s], preferred_element_type=F32).astype(BF16)
         both = jnp.dot(dgu_t[...], routed_v[s], preferred_element_type=F32).T.astype(BF16)
-        ggu_v[s, 0] = both[:, :h]
-        ggu_v[s, 1] = both[:, h:]
-        for c in store(o):
-            c.start()
-
-    def rs2_copy(k, d):
-        cols = pl.ds(*parts[d])
+        gg_ref[r, :] = both[:, :h]
+        gu_ref[r, :] = both[:, h:]
+
+    def rs2_copy(k, d, p):
+        cols, size = pl.ds(*parts[d]), n_tok // RS_PIECES
+        r = pl.ds(p * size, size)
         return remote(
-            rs2_0.at[:, cols] if k == 0 else rs2.at[k - 1, :, cols], rs2.at[k, :, cols],
-            rs2_send.at[d, k], rs2_recv.at[d, k], expert=me, tensor=(right, left)[d],
+            rs2_0.at[r, cols] if k == 0 else rs2.at[k - 1, r, cols], rs2.at[k, r, cols],
+            rs2_send.at[d, k, p], rs2_recv.at[d, k, p], expert=me, tensor=(right, left)[d],
         )
 
     def rs2_step(u):
@@ -419,20 +408,22 @@
             wait_bytes(ret.at[0, pl.ds(0, rows - cap), cols], push_recv.at[d, u])
             chosen = jnp.dot(pick[...], ret[o, :, cols], preferred_element_type=F32)
             mix_v[:, cols] = w_col_ref[:, 0:1] * chosen[:n_tok] + w_col_ref[:, 1:2] * chosen[n_tok:]
-        for d in range(2):
-            cols = pl.ds(*parts[d])
-            part = mix_v[:, cols]
-            if u == 0:
-                rs2_0[:, cols] = part.astype(BF16)
-            else:
-                rs2_copy(u - 1, d).wait_recv()
-                part = rs2[u - 1, :, cols].astype(F32) + part
+        for p in range(RS_PIECES):
+            r = pl.ds(p * (n_tok // RS_PIECES), n_tok // RS_PIECES)
+            for d in range(2):
+                cols = pl.ds(*parts[d])
+                part = mix_v[r, cols]
+                if u == 0:
+                    rs2_0[r, cols] = part.astype(BF16)
+                else:
+                    rs2_copy(u - 1, d, p).wait_recv()
+                    part = rs2[u - 1, r, cols].astype(F32) + part
+                    if u < nz - 1:
+                        rs2[u - 1, r, cols] = part.astype(BF16)
+                    else:
+                        mixed_ref[r, cols] = part.astype(BF16)
                 if u < nz - 1:
-                    rs2[u - 1, :, cols] = part.astype(BF16)
-                else:
-                    mixed_ref[:, cols] = part.astype(BF16)
-            if u < nz - 1:
-                go(rs2_copy(u, d))
+                    go(rs2_copy(u, d, p))
 
     def route_part():
         wait_bytes(dret.at[pl.ds(0, rows - cap)], d_recv)
@@ -476,16 +467,17 @@
                     return 0
 
                 lax.fori_loop(0, count, push_grad, 0)
-        grads(k - 1)
-        if k == 2:
+        if k <= 2:
+            grads(k - 1)
+        if k >= 2:
+            grads(k)
+        if k == 4:
             route_part()
         if k >= RS2_LAG:
             rs2_step(k - RS2_LAG)
     gret[slab(me), :] = islots[slab(me), :]
     for u in range(nz - RS2_LAG, nz - 1):
         rs2_step(u)
-        if u == nz - RS2_LAG:
-            grads(nz - 1)
     wait_bytes(gret.at[pl.ds(0, rows - cap)], g_recv)
     chosen = jnp.dot(pick[...], gret[...], preferred_element_type=F32)
     gtok_ref[...] = (w_col_ref[:, 0:1] * chosen[:n_tok] + w_col_ref[:, 1:2] * chosen[n_tok:]).astype(BF16)
@@ -497,9 +489,6 @@
         total = total + dsum[z]
     groute_ref[...] = total[0:2, :] / w_row_ref[...]
 
-    for o in (nz - 2, nz - 1):
-        for c in store(o):
-            c.wait()
     for c in started:
         c.wait_send()
     for d in range(2):
@@ -516,17 +505,17 @@
     h = wg.shape[1]
     rows = nx * cap
     dma = pltpu.SemaphoreType.DMA
-    small = jax.ShapeDtypeStruct((n_tok, width), BF16)
-    tall = jax.ShapeDtypeStruct((nz * width, h), BF16)
+    small = pltpu.VMEM((n_tok, width), BF16)
+    tall = pltpu.VMEM((nz * width, h), BF16)
     buffer = jax.ShapeDtypeStruct((nz, rows, width), BF16)
     return pl.pallas_call(
         functools.partial(layer_kernel, nx, nz, cap),
         out_shape=(
-            buffer, buffer, small, small, jax.ShapeDtypeStruct((2, n_tok), F32), tall, tall,
-            jax.ShapeDtypeStruct((h, nz * width), BF16),
+            buffer, buffer, small, small, pltpu.VMEM((2, n_tok), F32), tall, tall,
+            pltpu.VMEM((h, nz * width), BF16),
         ),
         in_specs=[VMEM] * 4 + [ANY] * 3,
-        out_specs=(ANY, ANY, VMEM, VMEM, VMEM, ANY, ANY, ANY),
+        out_specs=(ANY, ANY, VMEM, VMEM, VMEM, VMEM, VMEM, VMEM),
         scratch_shapes=[
             pltpu.VMEM((nz * width, h), BF16),
             pltpu.VMEM((nz * width, h), BF16),
@@ -558,17 +547,15 @@
             pltpu.VMEM((nz, 8, n_tok), F32),
             pltpu.VMEM((2, rows, width), BF16),
             pltpu.VMEM((2, rows, width), BF16),
-            pltpu.VMEM((2, 2, width, h), BF16),
-            pltpu.VMEM((2, h, width), BF16),
             dma((2, nz // 2, PIECES)), dma((2, nz // 2, PIECES)), dma((nz,)), dma((nz,)), dma((nz,)), dma, dma, dma,
             dma((2, nz - 1, PIECES)), dma((2, nz - 1, PIECES)), dma((2, 2, PIECES)), dma((3,)),
             dma((2, nz)), dma((2, nz)), dma((2, nz)),
             dma((2, nz - 1, RS_PIECES)), dma((2, nz - 1, RS_PIECES)),
-            dma, dma, dma((2, nz - 1)), dma((2, nz - 1)),
-            dma, dma, dma, dma, dma((2, 2)), dma((3, 2)),
+            dma, dma, dma((2, nz - 1, RS_PIECES)), dma((2, nz - 1, RS_PIECES)),
+            dma, dma, dma, dma, dma((2, 2)),
         ],
         compiler_params=pltpu.CompilerParams(
-            collective_id=0, has_side_effects=True, vmem_limit_bytes=62 * 1024 * 1024
+            collective_id=0, has_side_effects=True, vmem_limit_bytes=52 * 1024 * 1024
         ),
         name="layer",
     )(ids_t, weights_t, tokens, cotangent, wg, wu, wd)
@@ -579,29 +566,19 @@
 
 def finish_kernel(*refs):
     n = 6
-    ins, outs, held, get, put = refs[:n], refs[n : 2 * n], refs[2 * n : 3 * n], refs[3 * n], refs[3 * n + 1]
-
-    def pieces():
-        at = 0
-        for a, (src, dst, v) in enumerate(zip(ins, outs, held)):
-            axis = 0 if src.shape[0] >= src.shape[1] else 1
-            size = src.shape[axis] // CHUNKS if max(src.shape) >= 1024 * CHUNKS else src.shape[axis]
-            for c in range(src.shape[axis] // size):
-                where = (pl.ds(c * size, size), slice(None)) if axis == 0 else (slice(None), pl.ds(c * size, size))
-                yield (
-                    pltpu.make_async_copy(src.at[where], v.at[where], get.at[at]),
-                    pltpu.make_async_copy(v.at[where], dst.at[where], put.at[at]),
-                )
-                at += 1
-
-    moves = list(pieces())
-    for load, _ in moves:
-        load.start()
-    for load, store in moves:
-        load.wait()
-        store.start()
-    for _, store in moves:
-        store.wait()
+    ins, outs, put = refs[:n], refs[n : 2 * n], refs[2 * n]
+    moves = []
+    for src, dst in zip(ins, outs):
+        axis = 0 if src.shape[0] >= src.shape[1] else 1
+        count = CHUNKS if max(src.shape) >= 1024 * CHUNKS else 1
+        size = src.shape[axis] // count
+        for c in range(count):
+            where = (pl.ds(c * size, size), slice(None)) if axis == 0 else (slice(None), pl.ds(c * size, size))
+            moves.append(pltpu.make_async_copy(src.at[where], dst.at[where], put.at[len(moves)]))
+    for move in moves:
+        move.start()
+    for move in moves:
+        move.wait()
 
 
 def finish(*arrays):
@@ -610,11 +587,10 @@
     return pl.pallas_call(
         finish_kernel,
         out_shape=shapes,
-        in_specs=[ANY] * n,
+        in_specs=[VMEM] * n,
         out_specs=(ANY,) * n,
-        scratch_shapes=[pltpu.VMEM(a.shape, a.dtype) for a in arrays]
-        + [pltpu.SemaphoreType.DMA((n * CHUNKS,)), pltpu.SemaphoreType.DMA((n * CHUNKS,))],
-        compiler_params=pltpu.CompilerParams(vmem_limit_bytes=62 * 1024 * 1024),
+        scratch_shapes=[pltpu.SemaphoreType.DMA((n * CHUNKS,))],
+        compiler_params=pltpu.CompilerParams(vmem_limit_bytes=16 * 1024 * 1024),
         name="finish",
     )(*arrays)
 

time: 218 us -> 214 us (0.982)
  Pallas kernels: 216 us -> 213 us
    pallas_call x1, Pallas kernels: 5.46 us -> 2.77 us  [finish(): pl.pallas_call(finish_kernel, out_shape=shapes, in_specs=[VMEM] * n, out_...]
where the time goes in v4:
time: 214 us; the launch traced here: 213 us
  Pallas kernels  213 us (100%)
    pallas_call x1, Pallas kernels, layer(): pl.pallas_call(functools.partial(layer_kernel, nx, nz, cap), out_shape=(b...  210 us

profile of v4, /device:TPU:2, one launch (start us, length us, event | category | flops | bytes accessed | tf_op | source)
XLA Modules:
  0.0 213.5 jit_solution(14108935193119741594)
XLA Ops:
  0.6 209.9 %layer.1 = (bf16[8,512,896]{2,1,0:T(8,128)(2,1)}, bf16[8,512,896]{2,1,0:T(8,128)(2,1)}, bf16[128,896]{1,0:T(8,128)(2,1)S(1)}, bf16[128,896]{1,0:T(8,128)(2,1)S(1...) custom-call(s32[2,128]{1,0:T(2,128)} %bitcast.12, ...), custom_call_target="tpu_custom_call" | custom-call | tf_op jit(solution)/shard_map/layer/pallas_call | solution.py:511
  210.5 2.8 %finish.1 = (bf16[128,896]{1,0:T(8,128)(2,1)}, bf16[128,896]{1,0:T(8,128)(2,1)}, f32[2,128]{1,0:T(2,128)}, bf16[7168,128]{1,0:T(8,128)(2,1)}, bf16[7168,128]{1,0:T(8,128)(2,1)}, /*index=5*/bf16[128,7168]{1,0:T(8,128)(2,1)}) custom-call(bf16[128,896]{1,0:T(8,128)(2,1)S(1)} %get-tuple-element.18.refs_0_, bf16[128,896]{1,0:T(8,128)(2,1)S(1)} %get-tuple-element.19.refs_1_, ...), custom_call_target="tpu_custom_call" | custom-call | tf_op jit(solution)/shard_map/finish/pallas_call | solution.py:587

commit v5 on v4

--- a/solution.py
+++ b/solution.py
@@ -360,10 +360,9 @@
         remote(dsrc.at[slab(q)], dret.at[slab(me)], d_send, d_recv, expert=q, tensor=t).start()
         return 0
 
-    fill_bk(0, at(-1), rs0)
-    fill_bk(1, at(1), rs0)
-    for p in range(RS_PIECES):
-        for d in range(2):
+    for d in range(2):
+        fill_bk(d, at((-1, 1)[d]), rs0)
+        for p in range(RS_PIECES):
             go(rs_copy(0, d, p))
     down(1)
     lax.fori_loop(1, nx, push_dots, 0)
@@ -445,6 +444,8 @@
             fill_bk(d, at((-1 - k, 1 + k)[d]), bk)
         if k + 1 < nz:
             down(k + 1)
+        if k == 1:
+            grads(0)
         for p in range(RS_PIECES):
             r = pl.ds(p * size, size)
             for d in range(2):
@@ -467,10 +468,7 @@
                     return 0
 
                 lax.fori_loop(0, count, push_grad, 0)
-        if k <= 2:
-            grads(k - 1)
-        if k >= 2:
-            grads(k)
+        grads(k)
         if k == 4:
             route_part()
         if k >= RS2_LAG:

time: 214 us -> 214 us (level)
  no operation moved by 1% of the time
where the time goes in v5:
time: 214 us; the launch traced here: 213 us
  Pallas kernels  213 us (100%)
    pallas_call x1, Pallas kernels, layer(): pl.pallas_call(functools.partial(layer_kernel, nx, nz, cap), out_shape=(b...  210 us

profile of v5, /device:TPU:2, one launch (start us, length us, event | category | flops | bytes accessed | tf_op | source)
XLA Modules:
  0.0 213.5 jit_solution(16882518776637838725)
XLA Ops:
  0.6 209.9 %layer.1 = (bf16[8,512,896]{2,1,0:T(8,128)(2,1)}, bf16[8,512,896]{2,1,0:T(8,128)(2,1)}, bf16[128,896]{1,0:T(8,128)(2,1)S(1)}, bf16[128,896]{1,0:T(8,128)(2,1)S(1...) custom-call(s32[2,128]{1,0:T(2,128)} %bitcast.12, ...), custom_call_target="tpu_custom_call" | custom-call | tf_op jit(solution)/shard_map/layer/pallas_call | solution.py:509
  210.5 2.8 %finish.1 = (bf16[128,896]{1,0:T(8,128)(2,1)}, bf16[128,896]{1,0:T(8,128)(2,1)}, f32[2,128]{1,0:T(2,128)}, bf16[7168,128]{1,0:T(8,128)(2,1)}, bf16[7168,128]{1,0:T(8,128)(2,1)}, /*index=5*/bf16[128,7168]{1,0:T(8,128)(2,1)}) custom-call(bf16[128,896]{1,0:T(8,128)(2,1)S(1)} %get-tuple-element.18.refs_0_, bf16[128,896]{1,0:T(8,128)(2,1)S(1)} %get-tuple-element.19.refs_1_, ...), custom_call_target="tpu_custom_call" | custom-call | tf_op jit(solution)/shard_map/finish/pallas_call | solution.py:585
